TPU v7x, 256 devices: a whole 4x4x8 slice. The times are simulated.
256 devices in a mesh: tile: 32 (over z, x), mem: 8 (over y, core).
Axes of the slice: x: 4, y: 4, z: 8, core: 2. Of those that a mesh axis runs over, the one named last changes fastest.
Arguments:
- ensemble: bfloat16 [64, 512, 1024], P('mem', 'tile'), may hold values from -8 to 8
- obs_members: bfloat16 [32768, 64, 128], P(('tile', 'mem')), may hold values from -6 to 6
- obs_values: float32 [32768, 128], P(('tile', 'mem')), may hold values from -9 to 9
- obs_weight: float32 [32768, 128], P(('tile', 'mem')), may hold values from 0.05 to 1
- obs_count: int32 [32768], P(('tile', 'mem')), may hold values from 1 to 128
- obs_tile: int32 [32768], P(('tile', 'mem')), may hold values from 0 to 31, as said below
- obs_block: int32 [32768], P(('tile', 'mem')), may hold values from 0 to 15
- obs_turn: int32 [32768], P(('tile', 'mem')), may hold values from 0 to 3
Outputs:
- analysis_pert: bfloat16 [64, 512, 1024], P('mem', 'tile')
- analysis_mean: bfloat16 [512, 1024], P(('tile', 'mem'))
Inputs may be any that keep to these rules, and one draw needn't show every extreme that they name: `obs_tile`: within each aligned group of 128 consecutive blocks (the blocks of one device), no tile is named more than 8 times, and one tile is named exactly 8 times by every group.
All inputs are finite; a program needn't handle non-finite values.
Results may differ from a plain program's by a relative error of at most 0.0036.
Values may be sent and summed in bfloat16 or wider, within the bound.
A program may use at most 64 MiB of HBM per device.

v0:
```python
import jax
import jax.numpy as jnp
import numpy as np
from jax import lax
from jax.sharding import PartitionSpec as P

MEMBERS = 64
BPS = 4
OBD = 128
NS_STEPS = 6
ABLK = 16


def in_blocks(value, dim, count):
    before, after = (value.shape[:dim], value.shape[dim + 1 :])
    return jnp.moveaxis(value.reshape(*before, count, -1, *after), dim, 0)


def sent_and_summed(value, axis, dim):
    blocks = in_blocks(value, dim, lax.axis_size(axis))
    arrived = lax.all_to_all(blocks, axis, split_axis=0, concat_axis=0, tiled=True)
    return arrived.sum(axis=0)


def sent_together(arrays, axis, dim, along):
    columns = [a.reshape(*a.shape[:along], -1) for a in arrays]
    both = jnp.concatenate(columns, axis=along)
    whole, at, gathered = (sent_and_summed(both, axis, dim), 0, [])
    for a, column in zip(arrays, columns):
        share = whole[..., at : at + column.shape[along]]
        gathered.append(share.reshape(*share.shape[:along], *a.shape[along:]))
        at += column.shape[along]
    return tuple(gathered)


def product(left, right):
    return jnp.matmul(left, right, precision=lax.Precision.HIGHEST)


def target_block(obs_block, obs_turn):
    block_row = obs_block // BPS
    block_col = obs_block % BPS
    last = BPS - 1
    new_row = jnp.where(
        obs_turn == 0,
        block_row,
        jnp.where(
            obs_turn == 1, block_col, jnp.where(obs_turn == 2, last - block_row, last - block_col)
        ),
    )
    new_col = jnp.where(
        obs_turn == 0,
        block_col,
        jnp.where(
            obs_turn == 1, last - block_row, jnp.where(obs_turn == 2, last - block_col, block_row)
        ),
    )
    return new_row * BPS + new_col


def scaled_obs(obs_members, obs_values, obs_weight, obs_count):
    obs_mean = jnp.sum(obs_members, axis=1, dtype=jnp.float32) / MEMBERS
    usable = lax.broadcasted_iota(jnp.int32, obs_weight.shape, 1) < obs_count[:, None]
    weight_root = jnp.sqrt(jnp.where(usable, obs_weight, jnp.zeros_like(obs_weight)))
    scaled_pert = (
        (obs_members.astype(jnp.float32) - obs_mean[:, None, :]) * weight_root[:, None, :]
    ).astype(jnp.bfloat16)
    scaled_innov = ((obs_values - obs_mean) * weight_root).astype(jnp.bfloat16)
    return (scaled_pert, scaled_innov)


def transforms(gram, projection):
    identity = jnp.eye(MEMBERS, dtype=jnp.float32)
    system = (MEMBERS - 1.0) * identity + gram
    frob = jnp.sqrt(jnp.sum(system * system, axis=(1, 2)))[:, None, None]
    square_root = system / frob
    inverse = jnp.broadcast_to(identity, system.shape)
    for sweep in range(NS_STEPS):
        middle = 1.5 * identity - 0.5 * product(inverse, square_root)
        square_root = product(square_root, middle)
        inverse = product(middle, inverse)
    inverse_root = inverse / jnp.sqrt(frob)
    covariance = product(inverse_root, inverse_root)
    mean_weights = jnp.einsum(
        "bjk,bk->bj", covariance, projection, precision=lax.Precision.HIGHEST
    ).astype(jnp.bfloat16)
    spread = (jnp.sqrt(MEMBERS - 1.0) * inverse_root).astype(jnp.bfloat16)
    return (spread, mean_weights)


def triangle_tables(members):
    upper_row, upper_col = np.triu_indices(members)
    packed_flat = (upper_row * members + upper_col).astype(np.int32)
    lookup = np.zeros((members, members), np.int32)
    lookup[upper_row, upper_col] = np.arange(upper_row.shape[0], dtype=np.int32)
    lookup[upper_col, upper_row] = np.arange(upper_row.shape[0], dtype=np.int32)
    return (packed_flat, lookup.reshape(-1))


def body(ensemble, obs_members, obs_values, obs_weight, obs_count, obs_tile, obs_block, obs_turn):
    tile_count = lax.axis_size("tile")
    capacity = max(2, 2 * OBD // tile_count)
    slot_count = tile_count * capacity
    scaled_pert, scaled_innov = scaled_obs(obs_members, obs_values, obs_weight, obs_count)
    target = target_block(obs_block, obs_turn)
    later = lax.broadcasted_iota(jnp.int32, (OBD, OBD), 0) > lax.broadcasted_iota(
        jnp.int32, (OBD, OBD), 1
    )
    same_tile = obs_tile[:, None] == obs_tile[None, :]
    arrival = jnp.sum((later & same_tile).astype(jnp.int32), axis=1)
    position = obs_tile * capacity + arrival
    packed_flat, lookup = triangle_tables(MEMBERS)
    entries = packed_flat.shape[0]
    padded_width = (entries + 127) // 128 * 128
    own_gram = jnp.einsum(
        "nkr,nlr->nkl", scaled_pert, scaled_pert, preferred_element_type=jnp.float32
    )
    own_proj = jnp.einsum(
        "nkr,nr->nk", scaled_pert, scaled_innov, preferred_element_type=jnp.float32
    )
    packed = jnp.take(own_gram.reshape(OBD, MEMBERS * MEMBERS), jnp.asarray(packed_flat), axis=1)
    packed = jnp.pad(packed, ((0, 0), (0, padded_width - entries)))
    send_packed = jnp.zeros((slot_count, padded_width), jnp.float32).at[position].set(packed)
    send_proj = jnp.zeros((slot_count, MEMBERS), jnp.float32).at[position].set(own_proj)
    send_target = (
        jnp.zeros((slot_count, 1), jnp.float32)
        .at[position]
        .set(target.astype(jnp.float32)[:, None])
    )
    got_packed, slot_proj, got_target = (
        lax.all_to_all(send_packed, "tile", split_axis=0, concat_axis=0, tiled=True),
        lax.all_to_all(send_proj, "tile", split_axis=0, concat_axis=0, tiled=True),
        lax.all_to_all(send_target, "tile", split_axis=0, concat_axis=0, tiled=True),
    )
    slot_gram = jnp.take(got_packed, jnp.asarray(lookup), axis=1).reshape(
        slot_count, MEMBERS, MEMBERS
    )
    block_ids = jnp.arange(ABLK, dtype=jnp.float32)[None, :]
    belongs = (got_target == block_ids).astype(jnp.float32)
    gram = jnp.einsum("sb,skl->bkl", belongs, slot_gram, precision=lax.Precision.HIGHEST)
    projection = jnp.einsum("sb,sk->bk", belongs, slot_proj, precision=lax.Precision.HIGHEST)
    gram, projection = sent_together((gram, projection), "mem", 0, 2)
    spread, mean_weights = transforms(gram, projection)
    columns = lax.all_to_all(ensemble, "mem", split_axis=1, concat_axis=0, tiled=True)
    background_mean = jnp.sum(columns, axis=0, dtype=jnp.float32) / MEMBERS
    perturbation = (columns.astype(jnp.float32) - background_mean[None]).astype(jnp.bfloat16)
    analysis = jnp.einsum(
        "jbx,bjk->kbx", perturbation, spread, preferred_element_type=jnp.float32
    ).astype(jnp.bfloat16)
    increment = jnp.einsum(
        "jbx,bj->bx", perturbation, mean_weights, preferred_element_type=jnp.float32
    )
    block_mean = (background_mean + increment).astype(jnp.bfloat16)[None]
    analysis_pert = lax.all_to_all(analysis, "mem", split_axis=0, concat_axis=1, tiled=True)
    return (analysis_pert, block_mean[0])


def solution(mesh):
    placed = (
        P("mem", "tile", None),
        P(("tile", "mem"), None, None),
        P(("tile", "mem"), None),
        P(("tile", "mem"), None),
        P(("tile", "mem")),
        P(("tile", "mem")),
        P(("tile", "mem")),
        P(("tile", "mem")),
    )
    return jax.shard_map(
        body,
        mesh=mesh,
        in_specs=placed,
        out_specs=(P("mem", "tile", None), P(("tile", "mem"), None)),
        check_vma=False,
    )
```

profile of v0, /device:TPU:1, one launch (start us, length us, event | category | flops | bytes accessed | tf_op | source)
XLA Modules:
  0.0 168.5 jit_solution(13894121671265122537)
XLA Ops:
  0.7 1.0 convert_reduce_fusion.2
  1.7 0.7 compare_select_fusion
  2.4 1.0 scatter_custom_fusion
  3.4 0.7 all_to_all.45
  4.0 11.9 %all-to-all-start = ((f32[32,8,1]{1,2,0:T(1,128)}), f32[32,8,1]{1,2,0:T(1,128)S(1)}, u32[]{:S(2)}, u32[]{:S(2)}) async-start(f32[32,8,1]{1,2,0:T(1,128)} %bitcast), calls=%async_computation | async-start | bytes 32768 | tf_op jit(solution)/shard_map/all_to_all | solution.py:133
  15.9 2.2 %convert_reduce_fusion = f32[128,128]{1,0:T(8,128)S(1)} fusion(bf16[128,64,128]{2,1,0:T(8,128)(2,1)} %param.11), kind=kLoop, calls=%fused_computation.6 | loop fusion | flops 2080768 | bytes 2162688 | tf_op jit(solution)/shard_map/reduce_sum | solution.py:62
  18.2 0.9 fusion.26
  19.1 1.2 fusion.2
  20.3 0.9 scatter_custom_fusion.2
  21.2 0.8 reshape.191
  22.0 2.5 %all-to-all-done = f32[32,8,1]{1,2,0:T(1,128)S(1)} async-done(((f32[32,8,1]{1,2,0:T(1,128)}), f32[32,8,1]{1,2,0:T(1,128)S(1)}, u32[]{:S(2)}, u32[]{:S(2)}) %all-to-all-start) | async-done | bytes 1056 | tf_op jit(solution)/shard_map/all_to_all | solution.py:133
  24.5 6.7 %all-to-all-start.2 = ((f32[32,1,512]{2,1,0:T(1,128)}), f32[32,1,512]{2,1,0:T(1,128)S(1)}, u32[]{:S(2)}, u32[]{:S(2)}) async-start(f32[32,1,512]{2,1,0:T(1,128)} %reshape.191), calls=%async_computation.2 | async-start | bytes 131072 | tf_op jit(solution)/shard_map/all_to_all | solution.py:132
  31.2 3.2 %fusion.4 = f32[128,64,64]{2,1,0:T(8,128)} fusion(bf16[128,64,128]{2,1,0:T(8,128)(2,1)S(1)} %copy-done.1, f32[128,128]{1,0:T(8,128)S(1)} %get-tuple-element.3, f32[128,128]{1,0:T(8,128)S(1)} %get-tuple-element.4), kind=kOutput, calls=%fused_computation.10 | convolution fusion | flops 138412032 | bytes 4325376 | tf_op jit(solution)/shard_map/nkr,nlr->nkl/dot_general | solution.py:115
  34.4 3.8 %copy.71 = f32[128,64,64]{0,2,1:T(8,128)S(1)} copy(f32[128,64,64]{2,1,0:T(8,128)} %fusion.4) | data formatting | bytes 4194304 | tf_op jit(solution)/shard_map/nkr,nlr->nkl/dot_general | solution.py:115
  38.2 3.9 %gather_fusion = f32[2080,128]{1,0:T(8,128)S(1)} fusion(f32[128,4096]{0,1:T(8,128)S(1)} %bitcast.88, s32[3072]{0:T(1024)S(1)} %pad_clamp_fusion), kind=kCustom, calls=%fused_computation | custom fusion | bytes 2138240 | tf_op jit(solution)/shard_map/jit(_take)/gather | solution.py:121
  42.5 2.8 %scatter_custom_fusion.1 = f32[256,2176]{1,0:T(8,128)} fusion(s32[128]{0:T(128)S(1)} %get-tuple-element.7, f32[128,2080]{1,0:T(8,128)S(1)} %copy.98, f32[]{:T(128)} %constant.48.clone.1), kind=kCustom, calls=%fused_computation.26 | custom fusion | bytes 3343360 | tf_op jit(solution)/shard_map/scatter | solution.py:123
  45.4 9.4 %all-to-all-start.1 = ((f32[32,8,2176]{2,1,0:T(8,128)}), f32[32,8,2176]{2,1,0:T(8,128)S(1)}, u32[]{:S(2)}, u32[]{:S(2)}) async-start(f32[32,8,2176]{2,1,0:T(8,128)} %bitcast.91), calls=%async_computation.1 | async-start | bytes 4456448 | tf_op jit(solution)/shard_map/all_to_all | solution.py:131
  54.7 0.9 copy.78
  56.2 0.7 reduce.9
  57.5 0.8 reduce.10
  58.8 46.2 %all-to-all-done.1 = f32[32,8,2176]{2,1,0:T(8,128)S(1)} async-done(((f32[32,8,2176]{2,1,0:T(8,128)}), f32[32,8,2176]{2,1,0:T(8,128)S(1)}, u32[]{:S(2)}, u32[]{:S(2)}) %all-to-all-start.1) | async-done | bytes 2228256 | tf_op jit(solution)/shard_map/all_to_all | solution.py:131
  105.1 8.0 %all-to-all-start.4 = ((bf16[8,16,1024]{2,0,1:T(8,128)(2,1)}), bf16[8,16,1024]{2,0,1:T(8,128)(2,1)S(1)}, u32[]{:S(2)}, u32[]{:S(2)}) async-start(bf16[8,16,1024]{2,0,1:T(8,128)(2,1)} %copy.78), calls=%async_computation.4 | async-start | bytes 524288 | tf_op jit(solution)/shard_map/all_to_all | solution.py:144
  113.1 2.0 %copy.73 = f32[256,2176]{0,1:T(8,128)S(1)} copy(f32[256,2176]{1,0:T(8,128)} %bitcast.90) | data formatting | bytes 4456448 | tf_op jit(solution)/shard_map/all_to_all | solution.py:131
  115.1 16.1 %gather_fusion.1 = f32[4096,256]{1,0:T(8,128)} fusion(f32[256,2176]{0,1:T(8,128)S(1)} %copy.73, s32[4096]{0:T(1024)S(1)} %broadcast_clamp_fusion), kind=kCustom, calls=%fused_computation.1 | custom fusion | bytes 8404992 | tf_op jit(solution)/shard_map/jit(_take)/gather | solution.py:135
  131.2 4.8 %fusion.35 = f32[8,2,64,64]{3,0,2,1:T(8,128)S(1)} fusion(f32[256,64,64,1]{0,2,1,3:T(8,128)} %bitcast.89, f32[8,2]{0,1:T(2,128)S(1)} %multiply_add_fusion, f32[256]{0:T(256)S(1)} %eq.92), kind=kOutput, calls=%fused_computation.62 | convolution fusion | flops 201330688 | bytes 4457536 | tf_op jit(solution)/shard_map/sb,skl->bkl/dot_general | solution.py:140
  136.2 0.9 copy.76
  137.0 4.8 %all-to-all-start.3 = ((f32[8,2,64,65]{3,2,1,0:T(8,128)}), f32[8,2,64,65]{3,2,1,0:T(8,128)S(1)}, u32[]{:S(2)}, u32[]{:S(2)}) async-start(f32[8,2,64,65]{3,2,1,0:T(8,128)} %copy.76), calls=%async_computation.3 | async-start | bytes 1048576 | tf_op jit(solution)/shard_map/all_to_all | solution.py:21
  142.2 9.0 %all-to-all-done.3 = f32[8,2,64,65]{3,2,1,0:T(8,128)S(1)} async-done(((f32[8,2,64,65]{3,2,1,0:T(8,128)}), f32[8,2,64,65]{3,2,1,0:T(8,128)S(1)}, u32[]{:S(2)}, u32[]{:S(2)}) %all-to-all-start.3) | async-done | bytes 266272 | tf_op jit(solution)/shard_map/all_to_all | solution.py:21
  155.8 1.0 copy.82
  156.8 4.3 %all-to-all-start.5 = ((bf16[64,2,1024]{2,1,0:T(2,128)(2,1)}), bf16[64,2,1024]{2,1,0:T(2,128)(2,1)S(1)}, u32[]{:S(2)}, u32[]{:S(2)}) async-start(bf16[64,2,1024]{2,1,0:T(2,128)(2,1)} %copy.82), calls=%async_computation.5 | async-start | bytes 524288 | tf_op jit(solution)/shard_map/all_to_all | solution.py:154
  161.8 5.7 %all-to-all-done.5 = bf16[64,2,1024]{2,1,0:T(2,128)(2,1)S(1)} async-done(((bf16[64,2,1024]{2,1,0:T(2,128)(2,1)}), bf16[64,2,1024]{2,1,0:T(2,128)(2,1)S(1)}, u32[]{:S(2)}, u32[]{:S(2)}) %all-to-all-start.5) | async-done | bytes 262176 | tf_op jit(solution)/shard_map/all_to_all | solution.py:154
  167.7 0.8 all_to_all.58
  (60 shorter events, 8.0 us)
Async XLA Ops:
  0.6 18.5 %copy-start.1 = (bf16[128,64,128]{2,1,0:T(8,128)(2,1)S(1)}, bf16[128,64,128]{2,1,0:T(8,128)(2,1)}, u32[]{:S(2)}) copy-start(bf16[128,64,128]{2,1,0:T(8,128)(2,1)} %param.11) | copy-start | bytes 6291460
  0.6 17.5 %copy-start.3 = (f32[128,128]{1,0:T(8,128)S(1)}, f32[128,128]{1,0:T(8,128)}, u32[]{:S(2)}) copy-start(f32[128,128]{1,0:T(8,128)} %param.12) | copy-start | bytes 196612
  4.0 20.5 %all-to-all-start = ((f32[32,8,1]{1,2,0:T(1,128)}), f32[32,8,1]{1,2,0:T(1,128)S(1)}, u32[]{:S(2)}, u32[]{:S(2)}) async-start(f32[32,8,1]{1,2,0:T(1,128)} %bitcast), calls=%async_computation | async-start | bytes 32768 | tf_op jit(solution)/shard_map/all_to_all | solution.py:133
  24.5 20.8 %all-to-all-start.2 = ((f32[32,1,512]{2,1,0:T(1,128)}), f32[32,1,512]{2,1,0:T(1,128)S(1)}, u32[]{:S(2)}, u32[]{:S(2)}) async-start(f32[32,1,512]{2,1,0:T(1,128)} %reshape.191), calls=%async_computation.2 | async-start | bytes 131072 | tf_op jit(solution)/shard_map/all_to_all | solution.py:132
  34.4 3.8 %copy-start.5 = (s32[2080]{0:T(1024)S(1)}, s32[2080]{0:T(1024)}, u32[]{:S(2)}) copy-start(s32[2080]{0:T(1024)} %constant.124) | copy-start | bytes 24964
  45.4 9.4 %copy-start.2 = (bf16[8,16,1024]{2,1,0:T(8,128)(2,1)S(1)}, bf16[8,16,1024]{2,1,0:T(8,128)(2,1)}, u32[]{:S(2)}) copy-start(bf16[8,16,1024]{2,1,0:T(8,128)(2,1)} %param.10) | copy-start | bytes 786436
  45.4 10.3 %copy-start.4 = (s32[4096]{0:T(1024)S(1)}, s32[4096]{0:T(1024)}, u32[]{:S(2)}) copy-start(s32[4096]{0:T(1024)} %constant.125) | copy-start | bytes 49156
  45.4 59.7 %all-to-all-start.1 = ((f32[32,8,2176]{2,1,0:T(8,128)}), f32[32,8,2176]{2,1,0:T(8,128)S(1)}, u32[]{:S(2)}, u32[]{:S(2)}) async-start(f32[32,8,2176]{2,1,0:T(8,128)} %bitcast.91), calls=%async_computation.1 | async-start | bytes 4456448 | tf_op jit(solution)/shard_map/all_to_all | solution.py:131
  105.1 8.0 %copy-start = (f32[32,8,2176]{2,1,0:T(8,128)}, f32[32,8,2176]{2,1,0:T(8,128)S(1)}, u32[]{:S(2)}) copy-start(f32[32,8,2176]{2,1,0:T(8,128)S(1)} %all-to-all-done.1) | copy-start | bytes 6684676
  105.1 32.0 %all-to-all-start.4 = ((bf16[8,16,1024]{2,0,1:T(8,128)(2,1)}), bf16[8,16,1024]{2,0,1:T(8,128)(2,1)S(1)}, u32[]{:S(2)}, u32[]{:S(2)}) async-start(bf16[8,16,1024]{2,0,1:T(8,128)(2,1)} %copy.78), calls=%async_computation.4 | async-start | bytes 524288 | tf_op jit(solution)/shard_map/all_to_all | solution.py:144
  137.0 14.2 %all-to-all-start.3 = ((f32[8,2,64,65]{3,2,1,0:T(8,128)}), f32[8,2,64,65]{3,2,1,0:T(8,128)S(1)}, u32[]{:S(2)}, u32[]{:S(2)}) async-start(f32[8,2,64,65]{3,2,1,0:T(8,128)} %copy.76), calls=%async_computation.3 | async-start | bytes 1048576 | tf_op jit(solution)/shard_map/all_to_all | solution.py:21
  156.8 10.8 %all-to-all-start.5 = ((bf16[64,2,1024]{2,1,0:T(2,128)(2,1)}), bf16[64,2,1024]{2,1,0:T(2,128)(2,1)S(1)}, u32[]{:S(2)}, u32[]{:S(2)}) async-start(bf16[64,2,1024]{2,1,0:T(2,128)(2,1)} %copy.82), calls=%async_computation.5 | async-start | bytes 524288 | tf_op jit(solution)/shard_map/all_to_all | solution.py:154
where the time goes:
time: 170 us; the launch traced here: 169 us
  waiting for transfers between devices  63.5 us (37%)
  starting transfers between devices  45 us (26%)
  local copies, waits for them, and re-layouts  37.8 us (22%)
  matrix products  13.6 us (8%)
  other arithmetic  7.65 us (4%)
    all_to_all x1, waiting for transfers between devices, body(): lax.all_to_all(send_packed, 'tile', split_axis=0, concat_axis=0, tiled=True)  46.2 us
    gather x1, local copies, waits for them, and re-layouts, body(): jnp.take(got_packed, jnp.asarray(lookup), axis=1)  16.1 us
    all_to_all x1, starting transfers between devices, body(): lax.all_to_all(send_target, 'tile', split_axis=0, concat_axis=0, tiled=True)  11.9 us
    all_to_all x1, starting transfers between devices, body(): lax.all_to_all(send_packed, 'tile', split_axis=0, concat_axis=0, tiled=True)  9.35 us
    all_to_all x1, waiting for transfers between devices, sent_and_summed(): lax.all_to_all(blocks, axis, split_axis=0, concat_axis=0, tiled=True)  9.03 us
    all_to_all x1, starting transfers between devices, body(): lax.all_to_all(ensemble, 'mem', split_axis=1, concat_axis=0, tiled=True)  8.01 us
    all_to_all x1, starting transfers between devices, body(): lax.all_to_all(send_proj, 'tile', split_axis=0, concat_axis=0, tiled=True)  6.69 us
    all_to_all x1, waiting for transfers between devices, body(): lax.all_to_all(analysis, 'mem', split_axis=0, concat_axis=1, tiled=True)  5.74 us
  transfers between devices with their start and end apart: 6, of which 4 were waited for; matrix products, arithmetic and copies ran while one was open for 29% of the time, Pallas kernels for 0%

commit v1 on v0

v1 whole, which is shorter than its diff:
```python
import functools

import jax
import jax.numpy as jnp
from jax import lax
from jax.experimental import pallas as pl
from jax.experimental.pallas import tpu as pltpu
from jax.sharding import PartitionSpec as P

MESH = pl.DeviceIdType.MESH
MEMBERS = 64
ROWS = 128
OBD = 128
NS_STEPS = 6
NX, NY, NZ = 4, 4, 8
PACKED = 17
F32, BF16 = jnp.float32, jnp.bfloat16
CHUNKS = 8


def iota(shape, dim):
    return lax.broadcasted_iota(jnp.int32, shape, dim)


def nt(left, right):
    return lax.dot_general(left, right, (((1,), (1,)), ((), ())), preferred_element_type=F32)


def split(value):
    high = value.astype(BF16)
    return high, (value - high.astype(F32)).astype(BF16)


def product(left, right):
    (lh, ll), (rh, rl) = split(left), split(right)
    dot = functools.partial(jnp.dot, preferred_element_type=F32)
    return dot(lh, rh) + (dot(lh, rl) + dot(ll, rh))


def cell_rows(tile, block, turn, z, x, y, c):
    row, col = block // 4, block % 4
    new_row = jnp.where(turn == 0, row, jnp.where(turn == 1, col, jnp.where(turn == 2, 3 - row, 3 - col)))
    new_col = jnp.where(turn == 0, col, jnp.where(turn == 1, 3 - row, jnp.where(turn == 2, 3 - col, row)))
    dy = (new_row + NY - y) & 3
    dc = (new_col // 2 + c) & 1
    half = new_col & 1
    dz = ((tile // 4) + NZ - z) & 7
    dx = ((tile & 3) + NX - x) & 3
    inner = jnp.where(half == 0, dy * 32 + dx * 8, dx * 32 + dy * 8) + dz
    return dc * 256 + half * 128 + inner


def transforms(packed):
    main, extra = packed[:16], packed[16:17]
    lane, sub = iota((16, 128), 1), iota((16, 128), 0)
    col = lane & 15
    back = pltpu.roll(main, 112, 1)
    far = pltpu.roll(main, 64, 1)
    far_back = pltpu.roll(back, 64, 1)
    zero = jnp.zeros_like(main)
    row_d = jnp.where((lane < 48) | ((lane < 64) & (col < sub)), main, zero)
    row_c = jnp.where(lane < 32, far, jnp.where((lane < 48) & (col > sub), back, zero))
    ba = pltpu.roll(main, 32, 1)
    row_b = jnp.where((lane < 16) | ((lane < 32) & (col < sub)), ba, zero)
    aa = pltpu.roll(main, 16, 1)
    row_a = jnp.where((lane < 16) & (col > sub), aa, zero)
    del far_back
    half = jnp.concatenate([row_a, row_b, row_c, row_d], axis=0)
    full = jnp.concatenate([half, jnp.zeros((64, 128), F32)], axis=0)
    both = (full + full.T)[:64, :64]
    diag = pltpu.roll(jnp.broadcast_to(extra, (8, 128)), 64, 1)[0:1, :64]
    eye = iota((64, 64), 0) == iota((64, 64), 1)
    system = both + jnp.where(eye, diag + (MEMBERS - 1.0), 0.0)
    frob = jnp.sqrt(jnp.sum(system * system, axis=(0, 1), keepdims=True))
    root = system / frob
    identity = jnp.where(eye, 1.0, 0.0)
    middle = 1.5 * identity - 0.5 * root
    inverse = middle
    root = product(root, middle)
    for sweep in range(1, NS_STEPS):
        middle = 1.5 * identity - 0.5 * product(inverse, root)
        if sweep < NS_STEPS - 1:
            root = product(root, middle)
        inverse = product(middle, inverse)
    inverse_root = inverse / jnp.sqrt(frob)
    projection = jnp.broadcast_to(extra[:, :64], (16, 64))
    weights = product(product(projection, inverse_root), inverse_root)
    spread = (jnp.sqrt(F32(MEMBERS - 1.0)) * inverse_root).astype(BF16)
    return jnp.concatenate([spread, weights.astype(BF16)], axis=0)


def kernel(
    ens_ref, members_ref, values_ref, weight_ref, count_ref, tile_ref, block_ref, turn_ref,
    out_ref, mean_ref,
    obs, ens_f, ens_s, ens_r, pert_s, root_s, flat, core_s, core_r, own, s1, r1, acc1, s2, r2, acc2,
    s3, r3, ana,
    load_sem, ens_ss, ens_rs, core_ss, core_rs, ss1, rs1, ss2, rs2, ss3, rs3, out_ss, out_rs, self_sem,
):
    t, m = lax.axis_index("tile"), lax.axis_index("mem")
    z, x, y, c = t // 4, t % 4, m // 2, m % 2

    def at_mem(step):
        return (t, lax.rem(m + step, 8))

    def at_core():
        return (t, y * 2 + 1 - c)

    def at_y(step):
        return (t, lax.rem(y + step, NY) * 2 + c)

    def at_x(step):
        return (z * 4 + lax.rem(x + step, NX), m)

    def at_z(step):
        return (lax.rem(z + step, NZ) * 4 + x, m)

    def remote(src, dst, send_sem, recv_sem, device):
        return pltpu.make_async_remote_copy(
            src_ref=src, dst_ref=dst, send_sem=send_sem, recv_sem=recv_sem, device_id=device, device_id_type=MESH
        )

    barrier = pltpu.get_barrier_semaphore()
    partners = [at_mem(s) for s in range(1, 8)] + [at_x(s) for s in range(1, NX)] + [at_z(s) for s in range(1, NZ)]
    for device in partners:
        pl.semaphore_signal(barrier, inc=1, device_id=device, device_id_type=MESH)

    per = OBD // CHUNKS
    loads = [
        pltpu.make_async_copy(members_ref.at[pl.ds(i * per, per)], obs.at[pl.ds(i * per, per)], load_sem.at[i])
        for i in range(CHUNKS)
    ]
    for load in loads:
        load.start()

    for j in range(8):
        for k in range(8):
            ens_f[j, pl.ds(k, 16, stride=8), :] = ens_ref[k, :, j * 128 : j * 128 + 128].astype(F32)
        ens_s[:, :, :, j * 128 : j * 128 + 128] = ens_f[j].reshape(8, 2, 8, 128).astype(BF16)

    pl.semaphore_wait(barrier, len(partners))
    ens_copies = [
        remote(ens_s.at[lax.rem(m + s, 8)], ens_r.at[m], ens_ss.at[s], ens_rs.at[s], at_mem(s)) for s in range(1, 8)
    ]
    for copy in ens_copies:
        copy.start()

    count = jnp.broadcast_to(count_ref[...].astype(F32), (OBD, OBD)).T
    usable = iota((OBD, ROWS), 1).astype(F32) < count
    root_s[...] = jnp.sqrt(jnp.where(usable, weight_ref[...], 0.0))

    lane, sub = iota((16, 128), 1), iota((16, 128), 0)
    col = lane & 15
    rolled_in = ((lane & 63) >= 48) & (col > sub)
    on_diag = (lane < 64) & (col == sub)

    def one_block(n):
        raw = obs[n].astype(F32)
        mean = jnp.sum(raw, axis=0, keepdims=True) / MEMBERS
        scale = root_s[pl.ds(n, 1), :]
        pert = ((raw - mean) * scale).astype(BF16)
        innov = ((values_ref[pl.ds(n, 1), :] - mean) * scale).astype(BF16)
        left = jnp.concatenate([pert, jnp.broadcast_to(innov, (16, ROWS))], axis=0)
        right = jnp.concatenate([pert, pert[:32], pert[:32]], axis=0)
        gram = nt(left, right)
        a, b, cc, d, p = gram[:16], gram[16:32], gram[32:48], gram[48:64], gram[64:65]
        rolled = pltpu.roll(jnp.where(lane < 64, cc, a), 16, 1)
        base = jnp.where(lane < 64, d, jnp.where(lane < 96, cc, b))
        flat[pl.ds(n, 16, stride=OBD), :] = jnp.where(rolled_in, rolled, base)
        four = jnp.where(lane < 16, a, jnp.where(lane < 32, b, jnp.where(lane < 48, cc, d)))
        diag = jnp.sum(jnp.where(on_diag, four, 0.0), axis=0, keepdims=True)
        flat[pl.ds(16 * OBD + n, 1), :] = jnp.where(lane[:1] < 64, p, pltpu.roll(diag, 64, 1))

    for i in range(CHUNKS):
        loads[i].wait()

        def two_blocks(n, carry, i=i):
            for u in range(4):
                one_block(i * per + n * 4 + u)
            return carry

        lax.fori_loop(0, per // 4, two_blocks, 0)

    rows = cell_rows(tile_ref[...], block_ref[...], turn_ref[...], z, x, y, c)
    ids = iota((256, OBD), 0)
    for_other = jnp.where(ids + 256 == rows, 1.0, 0.0).astype(BF16)
    for_self = jnp.where(ids == rows, 1.0, 0.0).astype(BF16)

    def to_cells(hot, keep):
        def pair(k, carry):
            at = pl.multiple_of(k * 256, 256)
            data = jnp.concatenate([flat[pl.ds(at, OBD), :], flat[pl.ds(at + OBD, OBD), :]], axis=1).astype(BF16)
            sums = jnp.dot(hot, data, preferred_element_type=F32)
            for u in range(2):
                keep(k * 2 + u, sums[:, u * 128 : u * 128 + 128])
            return carry

        lax.fori_loop(0, 8, pair, 0)
        data = flat[pl.ds(16 * OBD, OBD), :].astype(BF16)
        keep(16, jnp.dot(hot, data, preferred_element_type=F32))

    def keep_other(r, sums):
        for q in range(8):
            core_s[q, r] = sums[q * 32 : q * 32 + 32].astype(BF16)

    def keep_own(r, sums):
        for q in range(8):
            own[q, r] = sums[q * 32 : q * 32 + 32]

    order = [1, 5, 2, 6, 3, 7, 0, 4]
    to_cells(for_other, keep_other)
    core_copies = {q: remote(core_s.at[q], core_r.at[q], core_ss.at[q], core_rs.at[q], at_core()) for q in order}
    for q in order:
        core_copies[q].start()
    to_cells(for_self, keep_own)

    copies1 = {}
    for q in order:
        half, step = q // 4, q % 4
        core_copies[q].wait_recv()
        if step:
            s1[q] = (own[q] + core_r[q].astype(F32)).astype(BF16)
            copies1[q] = remote(s1.at[q], r1.at[q], ss1.at[q], rs1.at[q], at_x(step) if half else at_y(step))
            copies1[q].start()
        else:
            acc1[half] = own[q] + core_r[q].astype(F32)

    copies2 = {}
    for half in range(2):
        for step in (1, 3, 2):
            copies1[half * 4 + step].wait_recv()
        acc = acc1[half]
        for step in range(1, 4):
            acc = acc + r1[half * 4 + step].astype(F32)
        acc2[pl.ds(half * PACKED, PACKED)] = acc[:, 0:8]
        for step in (2, 1, 3):
            q = half * 4 + step
            s2[q] = acc[:, step * 8 : step * 8 + 8].astype(BF16)
            copies2[q] = remote(s2.at[q], r2.at[q], ss2.at[q], rs2.at[q], at_y(step) if half else at_x(step))
            copies2[q].start()

    for half in range(2):
        for step in (1, 3, 2):
            copies2[half * 4 + step].wait_recv()
        span = pl.ds(half * PACKED, PACKED)
        acc = acc2[span]
        for step in range(1, 4):
            acc = acc + r2[half * 4 + step].astype(F32)
        acc2[span] = acc

    copies3 = {}
    wide = acc2.reshape(2 * PACKED * 8, 128)

    def cell(half, step):
        return wide[pl.ds(half * PACKED * 8 + step, PACKED, stride=8), :]

    for step in (4, 3, 5, 2, 6, 1, 7):
        for half in range(2):
            s3[step, half, 0:PACKED] = cell(half, step).astype(BF16)
        copies3[step] = remote(s3.at[step], r3.at[step], ss3.at[step], rs3.at[step], at_z(step))
        copies3[step].start()

    for copy in ens_copies:
        copy.wait_recv()
    ens_r[m] = ens_s[m]
    for g in range(2):
        raw = ens_r[:, g].astype(F32).reshape(MEMBERS, 1024)
        mean = jnp.sum(raw, axis=0, keepdims=True) / MEMBERS
        pert_s[g, 0:MEMBERS] = raw - mean
        pert_s[g, MEMBERS : MEMBERS + 8] = jnp.broadcast_to(mean, (8, 1024))

    for step in (1, 7, 2, 6, 3, 5, 4):
        copies3[step].wait_recv()
    both = []
    for half in range(2):
        total = cell(half, 0)
        for step in range(1, NZ):
            total = total + r3[step, half, 0:PACKED].astype(F32)
        both.append(transforms(total))

    means = []
    for g in range(2):
        result = jnp.dot(both[g], pert_s[g, 0:MEMBERS].astype(BF16), preferred_element_type=F32)
        for k in range(8):
            ana[k, g] = result[k * 8 : k * 8 + 8].astype(BF16)
        means.append(pert_s[g, MEMBERS : MEMBERS + 1] + result[64:65])
    out_copies = [
        remote(
            ana.at[lax.rem(m + s, 8)], out_ref.at[m], out_ss.at[s], out_rs.at[s], at_mem(s)
        )
        for s in (4, 3, 5, 2, 6, 1, 7)
    ]
    for copy in out_copies:
        copy.start()
    mine = pltpu.make_async_copy(ana.at[m], out_ref.at[m], self_sem)
    mine.start()
    mean_ref[...] = jnp.concatenate(means, axis=0).astype(BF16)

    for copy in ens_copies:
        copy.wait_send()
    for some in (core_copies, copies1, copies2, copies3):
        for copy in some.values():
            copy.wait_send()
    for copy in out_copies:
        copy.wait()
    mine.wait()


def body(ensemble, obs_members, obs_values, obs_weight, obs_count, obs_tile, obs_block, obs_turn):
    vmem, dma = pltpu.VMEM, pltpu.SemaphoreType.DMA
    whole = pl.BlockSpec(memory_space=pltpu.VMEM)
    arrived, mean = pl.pallas_call(
        kernel,
        name="letkf",
        out_shape=(
            jax.ShapeDtypeStruct((8, 2, 8, 1024), BF16),
            jax.ShapeDtypeStruct((2, 1024), BF16),
        ),
        in_specs=[whole, pl.BlockSpec(memory_space=pl.ANY)] + [whole] * 6,
        out_specs=(whole, whole),
        scratch_shapes=[
            vmem((OBD, MEMBERS, ROWS), BF16),
            vmem((8, 128, 128), F32),
            vmem((8, 2, 8, 1024), BF16),
            vmem((8, 2, 8, 1024), BF16),
            vmem((2, MEMBERS + 8, 1024), F32),
            vmem((OBD, ROWS), F32),
            vmem((PACKED * OBD, 128), F32),
            vmem((8, PACKED, 32, 128), BF16),
            vmem((8, PACKED, 32, 128), BF16),
            vmem((8, PACKED, 32, 128), F32),
            vmem((8, PACKED, 32, 128), BF16),
            vmem((8, PACKED, 32, 128), BF16),
            vmem((2, PACKED, 32, 128), F32),
            vmem((8, PACKED, 8, 128), BF16),
            vmem((8, PACKED, 8, 128), BF16),
            vmem((2 * PACKED, 8, 128), F32),
            vmem((NZ, 2, 24, 128), BF16),
            vmem((NZ, 2, 24, 128), BF16),
            vmem((8, 2, 8, 1024), BF16),
            dma((CHUNKS,)),
            dma((8,)), dma((8,)),
            dma((8,)), dma((8,)),
            dma((8,)), dma((8,)),
            dma((8,)), dma((8,)),
            dma((8,)), dma((8,)),
            dma((8,)), dma((8,)),
            dma(()),
        ],
        compiler_params=pltpu.CompilerParams(
            collective_id=0, has_side_effects=True, vmem_limit_bytes=48 << 20
        ),
    )(
        ensemble,
        obs_members,
        obs_values,
        obs_weight,
        obs_count.reshape(1, OBD),
        obs_tile.reshape(1, OBD),
        obs_block.reshape(1, OBD),
        obs_turn.reshape(1, OBD),
    )
    analysis = jnp.transpose(arrived.reshape(16, 8, 1024), (1, 0, 2))
    return analysis, mean


def solution(mesh):
    placed = (
        P("mem", "tile", None),
        P(("tile", "mem"), None, None),
        P(("tile", "mem"), None),
        P(("tile", "mem"), None),
        P(("tile", "mem")),
        P(("tile", "mem")),
        P(("tile", "mem")),
        P(("tile", "mem")),
    )
    return jax.shard_map(
        body,
        mesh=mesh,
        in_specs=placed,
        out_specs=(P("mem", "tile", None), P(("tile", "mem"), None)),
        check_vma=False,
    )
```

time: 170 us -> 58.5 us (0.34)
  waiting for transfers between devices: 63.5 us -> 0 us
  Pallas kernels: 0 us -> 49.3 us
  starting transfers between devices: 45 us -> 0 us
  local copies, waits for them, and re-layouts: 37.8 us -> 8.27 us
  matrix products: 13.6 us -> 0 us
  other arithmetic: 7.65 us -> 0 us
    all_to_all x6 -> x0, waiting for transfers between devices: 63.5 us -> none  [the longest x1 46.2 us: body(): lax.all_to_all(send_packed, 'tile', split_axis=0, concat_axis=0, tiled=True)]
    pallas_call x0 -> x1, Pallas kernels: none -> 49.3 us  [body(): pl.pallas_call(kernel, name='letkf', out_shape=(jax.ShapeDtypeStruct((8,...]
    all_to_all x6 -> x0, starting transfers between devices: 45 us -> none  [the longest x1 11.9 us: body(): lax.all_to_all(send_target, 'tile', split_axis=0, concat_axis=0, tiled=True)]
    gather x2 -> x0, local copies, waits for them, and re-layouts: 20 us -> none  [the longest x1 16.1 us: body(): jnp.take(got_packed, jnp.asarray(lookup), axis=1)]
    dot_general x25 -> x0, matrix products: 13.6 us -> none  [the longest x1 4.78 us: body(): jnp.einsum('sb,skl->bkl', belongs, slot_gram, precision=lax.Precision.HIG...]
    unnamed x16 -> x17, local copies, waits for them, and re-layouts: 2.08 us -> 7.42 us
    scatter x3 -> x0, local copies, waits for them, and re-layouts: 4.71 us -> none  [the longest x1 2.81 us: body(): jnp.zeros((slot_count, padded_width), jnp.float32).at[position].set(packed)]
    all_to_all x6 -> x0, local copies, waits for them, and re-layouts: 4.7 us -> none  [the longest x1 2 us: body(): lax.all_to_all(send_packed, 'tile', split_axis=0, concat_axis=0, tiled=True)]
  transfers between devices with their start and end apart: 6 -> 0, of which waited for: 4 -> 0; matrix products, arithmetic and copies ran while one was open for 29% -> 0% of each run, Pallas kernels for 0% -> 0%
where the time goes in v1:
time: 58.5 us; the launch traced here: 58.3 us
  Pallas kernels  49.3 us (84%)
  local copies, waits for them, and re-layouts  8.27 us (14%)
  between operations  0.66 us (1%)
    pallas_call x1, Pallas kernels, body(): pl.pallas_call(kernel, name='letkf', out_shape=(jax.ShapeDtypeStruct((8,...  49.3 us
    unnamed x17, local copies, waits for them, and re-layouts  7.42 us

profile of v1, /device:TPU:1, one launch (start us, length us, event | category | flops | bytes accessed | tf_op | source)
XLA Modules:
  0.0 58.3 jit_solution(6481869285639032263)
XLA Ops:
  0.6 0.0 copy-start
  0.6 1.6 %copy-done = bf16[128,64,128]{2,1,0:T(8,128)(2,1)S(1)} copy-done((bf16[128,64,128]{2,1,0:T(8,128)(2,1)S(1)}, bf16[128,64,128]{2,1,0:T(8,128)(2,1)}, u32[]{:S(2)}) %copy-start) | copy-done | bytes 2097176
  2.2 0.0 copy-start.1
  2.2 0.9 %copy-done.1 = bf16[8,16,1024]{2,1,0:T(8,128)(2,1)S(1)} copy-done((bf16[8,16,1024]{2,1,0:T(8,128)(2,1)S(1)}, bf16[8,16,1024]{2,1,0:T(8,128)(2,1)}, u32[]{:S(2)}) %copy-start.1) | copy-done | bytes 262168
  3.2 0.0 copy-start.2
  3.2 0.8 %copy-done.2 = f32[128,128]{1,0:T(8,128)S(1)} copy-done((f32[128,128]{1,0:T(8,128)S(1)}, f32[128,128]{1,0:T(8,128)}, u32[]{:S(2)}) %copy-start.2) | copy-done | bytes 65560
  4.0 0.0 copy-start.3
  4.0 0.8 %copy-done.3 = f32[128,128]{1,0:T(8,128)S(1)} copy-done((f32[128,128]{1,0:T(8,128)S(1)}, f32[128,128]{1,0:T(8,128)}, u32[]{:S(2)}) %copy-start.3) | copy-done | bytes 65560
  4.9 0.0 copy-start.4
  4.9 0.7 %copy-done.4 = s32[128]{0:T(128)S(1)} copy-done((s32[128]{0:T(128)S(1)}, s32[128]{0:T(128)}, u32[]{:S(2)}) %copy-start.4) | copy-done | bytes 536
  5.5 0.0 copy-start.5
  5.5 0.7 %copy-done.5 = s32[128]{0:T(128)S(1)} copy-done((s32[128]{0:T(128)S(1)}, s32[128]{0:T(128)}, u32[]{:S(2)}) %copy-start.5) | copy-done | bytes 536
  6.2 0.0 copy-start.6
  6.2 0.7 %copy-done.6 = s32[128]{0:T(128)S(1)} copy-done((s32[128]{0:T(128)S(1)}, s32[128]{0:T(128)}, u32[]{:S(2)}) %copy-start.6) | copy-done | bytes 536
  6.8 0.0 copy-start.7
  6.8 0.7 %copy-done.7 = s32[128]{0:T(128)S(1)} copy-done((s32[128]{0:T(128)S(1)}, s32[128]{0:T(128)}, u32[]{:S(2)}) %copy-start.7) | copy-done | bytes 536
  7.5 49.3 %letkf.1 = (bf16[8,2,8,1024]{3,2,1,0:T(8,128)(2,1)S(1)}, bf16[2,1024]{1,0:T(2,128)(2,1)S(1)}) custom-call(bf16[8,16,1024]{2,1,0:T(8,128)(2,1)S(1)} %copy-done.1, bf16[128,64,128]{2,1,0:T(8,128)(2,1)S(1)} %copy-done, f32[128,128]{1,0:T(8,128)S(1)} %copy-done.2, f32[128,128]{1,0:T(8,128)S(1)} %copy-done.3, s32[1,128]{1,0:T(1,128)S(1)} %bitcast.9, ...), custom_call_target="tpu_custom_call" | custom-call | tf_op jit(solution)/shard_map/letkf/pallas_call | solution.py:311
  56.8 0.9 %copy.12 = bf16[16,8,1024]{2,0,1:T(8,128)(2,1)} copy(bf16[16,8,1024]{2,1,0:T(8,128)(2,1)S(1)} %bitcast.8) | data formatting | bytes 524288 | tf_op jit(solution)/shard_map/reshape | solution.py:362
  57.7 0.6 %copy.14 = bf16[2,1024]{1,0:T(2,128)(2,1)} copy(bf16[2,1024]{1,0:T(2,128)(2,1)S(1)} %get-tuple-element.9) | data formatting | bytes 8192
Async XLA Ops:
  0.6 1.6 %copy-start = (bf16[128,64,128]{2,1,0:T(8,128)(2,1)S(1)}, bf16[128,64,128]{2,1,0:T(8,128)(2,1)}, u32[]{:S(2)}) copy-start(bf16[128,64,128]{2,1,0:T(8,128)(2,1)} %members_ref.1) | copy-start | bytes 6291460
  2.2 0.9 %copy-start.1 = (bf16[8,16,1024]{2,1,0:T(8,128)(2,1)S(1)}, bf16[8,16,1024]{2,1,0:T(8,128)(2,1)}, u32[]{:S(2)}) copy-start(bf16[8,16,1024]{2,1,0:T(8,128)(2,1)} %ens_ref.1) | copy-start | bytes 786436
  3.2 0.8 %copy-start.2 = (f32[128,128]{1,0:T(8,128)S(1)}, f32[128,128]{1,0:T(8,128)}, u32[]{:S(2)}) copy-start(f32[128,128]{1,0:T(8,128)} %values_ref.1) | copy-start | bytes 196612
  4.0 0.8 %copy-start.3 = (f32[128,128]{1,0:T(8,128)S(1)}, f32[128,128]{1,0:T(8,128)}, u32[]{:S(2)}) copy-start(f32[128,128]{1,0:T(8,128)} %weight_ref.1) | copy-start | bytes 196612
  4.9 0.7 %copy-start.4 = (s32[128]{0:T(128)S(1)}, s32[128]{0:T(128)}, u32[]{:S(2)}) copy-start(s32[128]{0:T(128)} %param.12) | copy-start | bytes 1540
  5.5 0.7 %copy-start.5 = (s32[128]{0:T(128)S(1)}, s32[128]{0:T(128)}, u32[]{:S(2)}) copy-start(s32[128]{0:T(128)} %param.13) | copy-start | bytes 1540
  6.2 0.7 %copy-start.6 = (s32[128]{0:T(128)S(1)}, s32[128]{0:T(128)}, u32[]{:S(2)}) copy-start(s32[128]{0:T(128)} %param.14) | copy-start | bytes 1540
  6.8 0.7 %copy-start.7 = (s32[128]{0:T(128)S(1)}, s32[128]{0:T(128)}, u32[]{:S(2)}) copy-start(s32[128]{0:T(128)} %param.15) | copy-start | bytes 1540

commit v2 on v1

v2 whole, which is shorter than its diff:
```python
import functools

import jax
import jax.numpy as jnp
from jax import lax
from jax.experimental import pallas as pl
from jax.experimental.pallas import tpu as pltpu
from jax.sharding import PartitionSpec as P

MESH = pl.DeviceIdType.MESH
MEMBERS = 64
ROWS = 128
OBD = 128
NS_STEPS = 6
NX, NY, NZ = 4, 4, 8
PACKED = 17
F32, BF16 = jnp.float32, jnp.bfloat16
CHUNKS = 8
EARLY = 4


def iota(shape, dim):
    return lax.broadcasted_iota(jnp.int32, shape, dim)


def nt(left, right):
    return lax.dot_general(left, right, (((1,), (1,)), ((), ())), preferred_element_type=F32)


def cell_rows(tile, block, turn, z, x, y, c):
    row, col = block // 4, block % 4
    new_row = jnp.where(turn == 0, row, jnp.where(turn == 1, col, jnp.where(turn == 2, 3 - row, 3 - col)))
    new_col = jnp.where(turn == 0, col, jnp.where(turn == 1, 3 - row, jnp.where(turn == 2, 3 - col, row)))
    dy = (new_row + NY - y) & 3
    dc = (new_col // 2 + c) & 1
    half = new_col & 1
    dz = ((tile // 4) + NZ - z) & 7
    dx = ((tile & 3) + NX - x) & 3
    inner = jnp.where(half == 0, dy * 32 + dx * 8, dx * 32 + dy * 8) + dz
    return dc * 256 + half * 128 + inner


def beside(left, right):
    return jnp.where(iota(left.shape, 1) < 64, left, pltpu.roll(right, 64, 1))


def stacked(value):
    left = iota(value.shape, 1) < 64
    zero = jnp.zeros_like(value)
    return jnp.concatenate([jnp.where(left, value, zero), jnp.where(left, zero, value)], axis=0)


def product(left, right):
    dot = functools.partial(jnp.dot, preferred_element_type=F32)
    high = left.astype(BF16)
    low = (left - high.astype(F32)).astype(BF16)
    wide = stacked(right)
    wide_high = wide.astype(BF16)
    wide_low = (wide - wide_high.astype(F32)).astype(BF16)
    first = dot(jnp.concatenate([high, low], axis=1), jnp.concatenate([wide_high, wide_high], axis=0))
    return first + dot(high, wide_low)


def half_matrix(main):
    lane, sub = iota((16, 128), 1), iota((16, 128), 0)
    col = lane & 15
    back = pltpu.roll(main, 112, 1)
    far = pltpu.roll(main, 64, 1)
    ba = pltpu.roll(main, 32, 1)
    aa = pltpu.roll(main, 16, 1)
    zero = jnp.zeros_like(main)
    row_d = jnp.where((lane < 48) | ((lane < 64) & (col < sub)), main, zero)
    row_c = jnp.where(lane < 32, far, jnp.where((lane < 48) & (col > sub), back, zero))
    row_b = jnp.where((lane < 16) | ((lane < 32) & (col < sub)), ba, zero)
    row_a = jnp.where((lane < 16) & (col > sub), aa, zero)
    return jnp.concatenate([row_a, row_b, row_c, row_d], axis=0)


def inverse_roots(first, second):
    one, two = half_matrix(first[:16]), half_matrix(second[:16])
    flipped = jnp.concatenate([one, two], axis=0).T[:64]
    lane, sub = iota((64, 128), 1), iota((64, 128), 0)
    eye = (lane & 63) == sub
    extra = [jnp.broadcast_to(v[16:17], (8, 128)) for v in (first, second)]
    diag = jnp.where(iota((8, 128), 1) < 64, pltpu.roll(extra[0], 64, 1), extra[1])[0:1]
    system = beside(one, two) + flipped + jnp.where(eye, diag + (MEMBERS - 1.0), 0.0)
    squares = jnp.sum(system * system, axis=0, keepdims=True)
    left = iota((1, 128), 1) < 64
    frob = jnp.sqrt(
        jnp.where(
            left,
            jnp.sum(jnp.where(left, squares, 0.0), axis=1, keepdims=True),
            jnp.sum(jnp.where(left, 0.0, squares), axis=1, keepdims=True),
        )
    )
    root = system / frob
    identity = jnp.where(eye, 1.0, 0.0)
    middle = 1.5 * identity - 0.5 * root
    inverse = middle
    root = product(root, middle)
    for sweep in range(1, NS_STEPS):
        middle = 1.5 * identity - 0.5 * product(inverse, root)
        if sweep < NS_STEPS - 1:
            root = product(root, middle)
        inverse = product(middle, inverse)
    return inverse / jnp.sqrt(frob), beside(extra[0], extra[1])


def kernel(
    ens_hbm, members_hbm, values_hbm, weight_hbm, count_hbm, tile_hbm, block_hbm, turn_hbm,
    out_hbm, mean_hbm,
    ens_ref, values_ref, weight_ref, count_ref, tile_ref, block_ref, turn_ref, mean_ref,
    obs, ens_f, ens_s, ens_r, means, pert_s, root_s, flat_f, flat_s, flat_r, rows_s, rows_r,
    s1, r1, acc1, s2, r2, acc2, s3, r3, ana,
    load_sem, small_sem, ens_ss, ens_rs, flat_ss, flat_rs, ss1, rs1, ss2, rs2, ss3, rs3, out_ss, out_rs, own_sem,
):
    t, m = lax.axis_index("tile"), lax.axis_index("mem")
    z, x, y, c = t // 4, t % 4, m // 2, m % 2

    def at_mem(step):
        return (t, lax.rem(m + step, 8))

    def at_core():
        return (t, y * 2 + 1 - c)

    def at_y(step):
        return (t, lax.rem(y + step, NY) * 2 + c)

    def at_x(step):
        return (z * 4 + lax.rem(x + step, NX), m)

    def at_z(step):
        return (lax.rem(z + step, NZ) * 4 + x, m)

    def remote(src, dst, send_sem, recv_sem, device):
        return pltpu.make_async_remote_copy(
            src_ref=src, dst_ref=dst, send_sem=send_sem, recv_sem=recv_sem, device_id=device, device_id_type=MESH
        )

    per = OBD // CHUNKS

    def load(i):
        span = pl.ds(i * per, per)
        return pltpu.make_async_copy(members_hbm.at[span], obs.at[span], load_sem.at[i])

    small = [
        pltpu.make_async_copy(source, target, small_sem.at[i])
        for i, (source, target) in enumerate(
            (
                (weight_hbm, weight_ref),
                (count_hbm, count_ref),
                (values_hbm, values_ref),
                (tile_hbm, tile_ref),
                (block_hbm, block_ref),
                (turn_hbm, turn_ref),
                (ens_hbm, ens_ref),
            )
        )
    ]
    for copy in small[:3]:
        copy.start()
    for i in range(CHUNKS):
        load(i).start()
    for copy in small[3:]:
        copy.start()

    barrier = pltpu.get_barrier_semaphore()
    partners = [at_mem(s) for s in range(1, 8)] + [at_x(s) for s in range(1, NX)] + [at_z(s) for s in range(1, NZ)]
    for device in partners:
        pl.semaphore_signal(barrier, inc=1, device_id=device, device_id_type=MESH)

    for copy in small[:3]:
        copy.wait()
    count = jnp.broadcast_to(count_ref[...].astype(F32), (OBD, OBD)).T
    usable = iota((OBD, ROWS), 1).astype(F32) < count
    root_s[...] = jnp.sqrt(jnp.where(usable, weight_ref[...], 0.0))

    lane, sub = iota((16, 128), 1), iota((16, 128), 0)
    col = lane & 15
    rolled_in = ((lane & 63) >= 48) & (col > sub)
    on_diag = (lane < 64) & (col == sub)

    def one_block(n, u):
        raw = obs[n].astype(F32)
        mean = jnp.sum(raw, axis=0, keepdims=True) / MEMBERS
        scale = root_s[pl.ds(n, 1), :]
        pert = ((raw - mean) * scale).astype(BF16)
        innov = ((values_ref[pl.ds(n, 1), :] - mean) * scale).astype(BF16)
        left = jnp.concatenate([pert, jnp.broadcast_to(innov, (16, ROWS))], axis=0)
        right = jnp.concatenate([pert, pert[:32], pert[:32]], axis=0)
        gram = nt(left, right)
        a, b, cc, d, p = gram[:16], gram[16:32], gram[32:48], gram[48:64], gram[64:65]
        rolled = pltpu.roll(jnp.where(lane < 64, cc, a), 16, 1)
        base = jnp.where(lane < 64, d, jnp.where(lane < 96, cc, b))
        flat_f[pl.ds(u, 16, stride=per), :] = jnp.where(rolled_in, rolled, base)
        four = jnp.where(lane < 16, a, jnp.where(lane < 32, b, jnp.where(lane < 48, cc, d)))
        diag = jnp.sum(jnp.where(on_diag, four, 0.0), axis=0, keepdims=True)
        flat_f[16 * per + u : 16 * per + u + 1, :] = jnp.where(lane[:1] < 64, p, pltpu.roll(diag, 64, 1))

    def chunk(i):
        load(i).wait()
        for u in range(per):
            one_block(i * per + u, u)
        flat_s[i] = flat_f[...].reshape(PACKED, per, 128).astype(BF16)

    def flat_copy(i):
        return remote(flat_s.at[i], flat_r.at[i], flat_ss.at[i], flat_rs.at[i], at_core())

    def plain(i, carry):
        chunk(i)
        return carry

    def with_copy(i, carry):
        chunk(i)
        flat_copy(i).start()
        return carry

    lax.fori_loop(0, EARLY, plain, 0)

    for copy in small[3:]:
        copy.wait()
    rows = cell_rows(tile_ref[...], block_ref[...], turn_ref[...], z, x, y, c).astype(F32)
    rows_s[...] = jnp.broadcast_to(rows - 256.0, (8, OBD))
    for j in range(8):
        for k in range(8):
            ens_f[j, pl.ds(k, 16, stride=8), :] = ens_ref[k, :, j * 128 : j * 128 + 128].astype(F32)
        ens_s[:, :, :, j * 128 : j * 128 + 128] = ens_f[j].reshape(8, 2, 8, 128).astype(BF16)

    pl.semaphore_wait(barrier, len(partners))
    rows_copy = remote(rows_s, rows_r, flat_ss.at[CHUNKS], flat_rs.at[CHUNKS], at_core())
    rows_copy.start()
    for i in range(EARLY):
        flat_copy(i).start()
    ens_copies = [
        remote(ens_s.at[lax.rem(m + s, 8)], ens_r.at[m], ens_ss.at[s], ens_rs.at[s], at_mem(s)) for s in range(1, 8)
    ]
    for copy in ens_copies:
        copy.start()
    lax.fori_loop(EARLY, CHUNKS, with_copy, 0)

    rows_copy.wait_recv()
    for i in range(CHUNKS):
        flat_copy(i).wait_recv()
    ids = iota((256, OBD), 0).astype(F32)
    hot = jnp.concatenate(
        [jnp.where(ids == rows, 1.0, 0.0).astype(BF16), jnp.where(ids == rows_r[0:1], 1.0, 0.0).astype(BF16)], axis=1
    )

    def keep(r, sums):
        for q in range(8):
            part = sums[q * 32 : q * 32 + 32]
            if q % 4:
                s1[q, r] = part.astype(BF16)
            else:
                acc1[q // 4, r] = part

    def both_cores(r):
        return jnp.concatenate([flat_s[:, r].reshape(OBD, 128), flat_r[:, r].reshape(OBD, 128)], axis=0)

    def pair(k, carry):
        data = jnp.concatenate([both_cores(k * 2), both_cores(k * 2 + 1)], axis=1)
        sums = jnp.dot(hot, data, preferred_element_type=F32)
        for u in range(2):
            keep(k * 2 + u, sums[:, u * 128 : u * 128 + 128])
        return carry

    groups = ((0, 8), (8, 9))

    def copy1(q, g):
        span = pl.ds(*groups[g])
        at, step = q * 2 + g, q % 4
        device = at_x(step) if q >= 4 else at_y(step)
        return remote(s1.at[q, span], r1.at[q, span], ss1.at[at], rs1.at[at], device)

    def copy2(q, g):
        span = pl.ds(*groups[g])
        at, step = q * 2 + g, q % 4
        device = at_y(step) if q >= 4 else at_x(step)
        return remote(s2.at[q, span], r2.at[q, span], ss2.at[at], rs2.at[at], device)

    def copy3(step, g):
        span = pl.ds(*((0, 8), (8, 16))[g])
        at = step * 2 + g
        return remote(s3.at[step, :, span], r3.at[step, :, span], ss3.at[at], rs3.at[at], at_z(step))

    order = (2, 6, 1, 5, 3, 7)
    for g in range(2):
        lax.fori_loop(g * 4, g * 4 + 4, pair, 0)
        if g:
            keep(16, jnp.dot(hot, both_cores(16), preferred_element_type=F32))
        for q in order:
            copy1(q, g).start()

    for g, (start, size) in enumerate(groups):
        span = pl.ds(start, size)
        for half in range(2):
            for step in (1, 3, 2):
                copy1(half * 4 + step, g).wait_recv()
            acc = acc1[half, span]
            for step in range(1, 4):
                acc = acc + r1[half * 4 + step, span].astype(F32)
            acc2[pl.ds(half * PACKED + start, size)] = acc[:, 0:8]
            for step in (2, 1, 3):
                q = half * 4 + step
                s2[q, span] = acc[:, step * 8 : step * 8 + 8].astype(BF16)
                copy2(q, g).start()

    wide = acc2.reshape(2 * PACKED * 8, 128)

    def cell(half, step, start, size):
        return wide[pl.ds((half * PACKED + start) * 8 + step, size, stride=8), :]

    for g, (start, size) in enumerate(groups):
        for half in range(2):
            for step in (1, 3, 2):
                copy2(half * 4 + step, g).wait_recv()
            span = pl.ds(half * PACKED + start, size)
            acc = acc2[span]
            for step in range(1, 4):
                acc = acc + r2[half * 4 + step, pl.ds(start, size)].astype(F32)
            acc2[span] = acc
        for step in (4, 3, 5, 2, 6, 1, 7):
            for half in range(2):
                s3[step, half, start : start + size] = cell(half, step, start, size).astype(BF16)
            copy3(step, g).start()

    for copy in ens_copies:
        copy.wait_recv()
    ens_r[m] = ens_s[m]
    for g in range(2):
        raw = ens_r[:, g].astype(F32).reshape(MEMBERS, 1024)
        mean = jnp.sum(raw, axis=0, keepdims=True) / MEMBERS
        means[g : g + 1] = mean
        pert_s[g * MEMBERS : g * MEMBERS + MEMBERS] = (raw - mean).astype(BF16)

    for g in range(2):
        for step in (1, 7, 2, 6, 3, 5, 4):
            copy3(step, g).wait_recv()
    total = []
    for half in range(2):
        value = cell(half, 0, 0, PACKED)
        for step in range(1, NZ):
            value = value + r3[step, half, 0:PACKED].astype(F32)
        total.append(value)
    roots, projection = inverse_roots(*total)

    spread = (jnp.sqrt(F32(MEMBERS - 1.0)) * roots).astype(BF16)
    result = jnp.dot(stacked(spread), pert_s[...], preferred_element_type=F32)
    for g in range(2):
        for k in range(8):
            at = g * MEMBERS + k * 8
            ana[k, g] = result[at : at + 8].astype(BF16)
    out_copies = [
        remote(ana.at[lax.rem(m + s, 8)], out_hbm.at[m], out_ss.at[s], out_rs.at[s], at_mem(s))
        for s in (4, 3, 5, 2, 6, 1, 7)
    ]
    for copy in out_copies:
        copy.start()
    mine = pltpu.make_async_copy(ana.at[m], out_hbm.at[m], own_sem.at[0])
    mine.start()

    weights = product(product(projection, roots), roots).astype(BF16)
    rise = jnp.dot(stacked(weights), pert_s[...], preferred_element_type=F32)
    mean_ref[...] = (means[0:2] + jnp.concatenate([rise[0:1], rise[8:9]], axis=0)).astype(BF16)
    mean_copy = pltpu.make_async_copy(mean_ref, mean_hbm, own_sem.at[1])
    mean_copy.start()

    for copy in out_copies:
        copy.wait()
    mine.wait()
    mean_copy.wait()
    for copy in ens_copies:
        copy.wait_send()
    rows_copy.wait_send()
    for i in range(CHUNKS):
        flat_copy(i).wait_send()
    for g in range(2):
        for q in order:
            copy1(q, g).wait_send()
            copy2(q, g).wait_send()
        for step in range(1, NZ):
            copy3(step, g).wait_send()


def body(ensemble, obs_members, obs_values, obs_weight, obs_count, obs_tile, obs_block, obs_turn):
    vmem, dma = pltpu.VMEM, pltpu.SemaphoreType.DMA
    whole = pl.BlockSpec(memory_space=pl.ANY)
    per = OBD // CHUNKS
    arrived, mean = pl.pallas_call(
        kernel,
        name="letkf",
        out_shape=(
            jax.ShapeDtypeStruct((8, 2, 8, 1024), BF16),
            jax.ShapeDtypeStruct((2, 1024), BF16),
        ),
        in_specs=[whole] * 8,
        out_specs=(whole, whole),
        scratch_shapes=[
            vmem((8, 16, 1024), BF16),
            vmem((OBD, ROWS), F32),
            vmem((OBD, ROWS), F32),
            vmem((1, OBD), jnp.int32),
            vmem((1, OBD), jnp.int32),
            vmem((1, OBD), jnp.int32),
            vmem((1, OBD), jnp.int32),
            vmem((2, 1024), BF16),
            vmem((OBD, MEMBERS, ROWS), BF16),
            vmem((8, 128, 128), F32),
            vmem((8, 2, 8, 1024), BF16),
            vmem((8, 2, 8, 1024), BF16),
            vmem((8, 1024), F32),
            vmem((2 * MEMBERS, 1024), BF16),
            vmem((OBD, ROWS), F32),
            vmem((PACKED * per, 128), F32),
            vmem((CHUNKS, PACKED, per, 128), BF16),
            vmem((CHUNKS, PACKED, per, 128), BF16),
            vmem((8, OBD), F32),
            vmem((8, OBD), F32),
            vmem((8, PACKED, 32, 128), BF16),
            vmem((8, PACKED, 32, 128), BF16),
            vmem((2, PACKED, 32, 128), F32),
            vmem((8, PACKED, 8, 128), BF16),
            vmem((8, PACKED, 8, 128), BF16),
            vmem((2 * PACKED, 8, 128), F32),
            vmem((NZ, 2, 24, 128), BF16),
            vmem((NZ, 2, 24, 128), BF16),
            vmem((8, 2, 8, 1024), BF16),
            dma((CHUNKS,)), dma((7,)),
            dma((8,)), dma((8,)),
            dma((CHUNKS + 1,)), dma((CHUNKS + 1,)),
            dma((16,)), dma((16,)),
            dma((16,)), dma((16,)),
            dma((16,)), dma((16,)),
            dma((8,)), dma((8,)),
            dma((2,)),
        ],
        compiler_params=pltpu.CompilerParams(
            collective_id=0, has_side_effects=True, vmem_limit_bytes=67043328
        ),
    )(
        ensemble,
        obs_members,
        obs_values,
        obs_weight,
        obs_count.reshape(1, OBD),
        obs_tile.reshape(1, OBD),
        obs_block.reshape(1, OBD),
        obs_turn.reshape(1, OBD),
    )
    analysis = jnp.transpose(arrived.reshape(16, 8, 1024), (1, 0, 2))
    return analysis, mean


def solution(mesh):
    placed = (
        P("mem", "tile", None),
        P(("tile", "mem"), None, None),
        P(("tile", "mem"), None),
        P(("tile", "mem"), None),
        P(("tile", "mem")),
        P(("tile", "mem")),
        P(("tile", "mem")),
        P(("tile", "mem")),
    )
    return jax.shard_map(
        body,
        mesh=mesh,
        in_specs=placed,
        out_specs=(P("mem", "tile", None), P(("tile", "mem"), None)),
        check_vma=False,
    )
```

time: 58.5 us -> 44.7 us (0.76)
  Pallas kernels: 49.3 us -> 40.8 us
  local copies, waits for them, and re-layouts: 8.27 us -> 3.08 us
    pallas_call x1, Pallas kernels: 49.3 us -> 40.8 us  [body(): pl.pallas_call(kernel, name='letkf', out_shape=(jax.ShapeDtypeStruct((8,...]
    unnamed x17 -> x1, local copies, waits for them, and re-layouts: 7.42 us -> 1.28 us
    reshape x1, local copies, waits for them, and re-layouts: 0.85 us -> 1.8 us  [body(): analysis = jnp.transpose(arrived.reshape(16, 8, 1024), (1, 0, 2))]
where the time goes in v2:
time: 44.7 us; the launch traced here: 44.5 us
  Pallas kernels  40.8 us (91%)
  local copies, waits for them, and re-layouts  3.08 us (7%)
  between operations  0.64 us (1%)
    pallas_call x1, Pallas kernels, body(): pl.pallas_call(kernel, name='letkf', out_shape=(jax.ShapeDtypeStruct((8,...  40.8 us
    reshape x1, local copies, waits for them, and re-layouts, body(): analysis = jnp.transpose(arrived.reshape(16, 8, 1024), (1, 0, 2))  1.8 us
    unnamed x1, local copies, waits for them, and re-layouts  1.28 us

profile of v2, /device:TPU:1, one launch (start us, length us, event | category | flops | bytes accessed | tf_op | source)
XLA Modules:
  0.0 44.5 jit_solution(10816353479970295923)
XLA Ops:
  0.6 40.8 %letkf.1 = (bf16[8,2,8,1024]{3,2,1,0:T(8,128)(2,1)}, bf16[2,1024]{1,0:T(2,128)(2,1)}) custom-call(bf16[8,16,1024]{2,1,0:T(8,128)(2,1)} %ens_hbm.1, bf16[128,64,128]{2,1,0:T(8,128)(2,1)} %members_hbm.1, f32[128,128]{1,0:T(8,128)} %values_hbm.1, f32[128,128]{1,0:T(8,128)} %weight_hbm.1, s32[1,128]{1,0:T(1,128)} %bitcast.10, s32[1,128]{1,0:T(1,128)} %bitcast.11, ...), custom_call_target="tpu_custom_call" | custom-call | tf_op jit(solution)/shard_map/letkf/pallas_call | solution.py:389
  41.4 1.8 %copy.12 = bf16[16,8,1024]{2,0,1:T(8,128)(2,1)} copy(bf16[16,8,1024]{2,1,0:T(8,128)(2,1)} %bitcast.9) | data formatting | bytes 524288 | tf_op jit(solution)/shard_map/reshape | solution.py:450
  43.2 1.3 %copy.14 = bf16[2,1024]{1,0:T(2,128)(2,1)} copy(bf16[2,1024]{1,0:T(2,128)(2,1)} %get-tuple-element.9) | data formatting | bytes 8192

commit v3 on v2

--- a/solution.py
+++ b/solution.py
@@ -16,7 +16,8 @@
 PACKED = 17
 F32, BF16 = jnp.float32, jnp.bfloat16
 CHUNKS = 8
-EARLY = 4
+GROUPS = ((0, 6), (6, 6), (12, 5))
+EARLY = 5
 
 
 def iota(shape, dim):
@@ -101,8 +102,10 @@
     for sweep in range(1, NS_STEPS):
         middle = 1.5 * identity - 0.5 * product(inverse, root)
         if sweep < NS_STEPS - 1:
-            root = product(root, middle)
-        inverse = product(middle, inverse)
+            both = product(jnp.concatenate([root, inverse], axis=0), middle)
+            root, inverse = both[:64], both[64:]
+        else:
+            inverse = product(inverse, middle)
     return inverse / jnp.sqrt(frob), beside(extra[0], extra[1])
 
 
@@ -111,7 +114,7 @@
     out_hbm, mean_hbm,
     ens_ref, values_ref, weight_ref, count_ref, tile_ref, block_ref, turn_ref, mean_ref,
     obs, ens_f, ens_s, ens_r, means, pert_s, root_s, flat_f, flat_s, flat_r, rows_s, rows_r,
-    s1, r1, acc1, s2, r2, acc2, s3, r3, ana,
+    s1, r1, acc1, s2, r2, acc2, s3, r3, total, ana,
     load_sem, small_sem, ens_ss, ens_rs, flat_ss, flat_rs, ss1, rs1, ss2, rs2, ss3, rs3, out_ss, out_rs, own_sem,
 ):
     t, m = lax.axis_index("tile"), lax.axis_index("mem")
@@ -187,12 +190,12 @@
         pert = ((raw - mean) * scale).astype(BF16)
         innov = ((values_ref[pl.ds(n, 1), :] - mean) * scale).astype(BF16)
         left = jnp.concatenate([pert, jnp.broadcast_to(innov, (16, ROWS))], axis=0)
-        right = jnp.concatenate([pert, pert[:32], pert[:32]], axis=0)
-        gram = nt(left, right)
+        gram = jnp.concatenate([nt(left, pert), jnp.zeros((80, 64), F32)], axis=1)
         a, b, cc, d, p = gram[:16], gram[16:32], gram[32:48], gram[48:64], gram[64:65]
-        rolled = pltpu.roll(jnp.where(lane < 64, cc, a), 16, 1)
-        base = jnp.where(lane < 64, d, jnp.where(lane < 96, cc, b))
-        flat_f[pl.ds(u, 16, stride=per), :] = jnp.where(rolled_in, rolled, base)
+        upper = rolled_in & (lane < 64)
+        second = jnp.where(lane < 32, cc, jnp.where(upper, pltpu.roll(a, 48, 1), pltpu.roll(b, 32, 1)))
+        first = jnp.where(upper, pltpu.roll(cc, 16, 1), d)
+        flat_f[pl.ds(u, 16, stride=per), :] = jnp.where(lane < 64, first, pltpu.roll(second, 64, 1))
         four = jnp.where(lane < 16, a, jnp.where(lane < 32, b, jnp.where(lane < 48, cc, d)))
         diag = jnp.sum(jnp.where(on_diag, four, 0.0), axis=0, keepdims=True)
         flat_f[16 * per + u : 16 * per + u + 1, :] = jnp.where(lane[:1] < 64, p, pltpu.roll(diag, 64, 1))
@@ -264,34 +267,31 @@
             keep(k * 2 + u, sums[:, u * 128 : u * 128 + 128])
         return carry
 
-    groups = ((0, 8), (8, 9))
-
     def copy1(q, g):
-        span = pl.ds(*groups[g])
-        at, step = q * 2 + g, q % 4
+        span = pl.ds(*GROUPS[g])
+        at, step = q * len(GROUPS) + g, q % 4
         device = at_x(step) if q >= 4 else at_y(step)
         return remote(s1.at[q, span], r1.at[q, span], ss1.at[at], rs1.at[at], device)
 
     def copy2(q, g):
-        span = pl.ds(*groups[g])
-        at, step = q * 2 + g, q % 4
+        span = pl.ds(*GROUPS[g])
+        at, step = q * len(GROUPS) + g, q % 4
         device = at_y(step) if q >= 4 else at_x(step)
         return remote(s2.at[q, span], r2.at[q, span], ss2.at[at], rs2.at[at], device)
 
     def copy3(step, g):
-        span = pl.ds(*((0, 8), (8, 16))[g])
-        at = step * 2 + g
-        return remote(s3.at[step, :, span], r3.at[step, :, span], ss3.at[at], rs3.at[at], at_z(step))
+        at = step * len(GROUPS) + g
+        return remote(s3.at[step, g], r3.at[step, g], ss3.at[at], rs3.at[at], at_z(step))
 
     order = (2, 6, 1, 5, 3, 7)
-    for g in range(2):
-        lax.fori_loop(g * 4, g * 4 + 4, pair, 0)
-        if g:
+    for g, (start, size) in enumerate(GROUPS):
+        lax.fori_loop(start // 2, (start + size) // 2, pair, 0)
+        if size % 2:
             keep(16, jnp.dot(hot, both_cores(16), preferred_element_type=F32))
         for q in order:
             copy1(q, g).start()
 
-    for g, (start, size) in enumerate(groups):
+    for g, (start, size) in enumerate(GROUPS):
         span = pl.ds(start, size)
         for half in range(2):
             for step in (1, 3, 2):
@@ -310,7 +310,7 @@
     def cell(half, step, start, size):
         return wide[pl.ds((half * PACKED + start) * 8 + step, size, stride=8), :]
 
-    for g, (start, size) in enumerate(groups):
+    for g, (start, size) in enumerate(GROUPS):
         for half in range(2):
             for step in (1, 3, 2):
                 copy2(half * 4 + step, g).wait_recv()
@@ -321,7 +321,7 @@
             acc2[span] = acc
         for step in (4, 3, 5, 2, 6, 1, 7):
             for half in range(2):
-                s3[step, half, start : start + size] = cell(half, step, start, size).astype(BF16)
+                s3[step, g, half, 0:size] = cell(half, step, start, size).astype(BF16)
             copy3(step, g).start()
 
     for copy in ens_copies:
@@ -333,16 +333,15 @@
         means[g : g + 1] = mean
         pert_s[g * MEMBERS : g * MEMBERS + MEMBERS] = (raw - mean).astype(BF16)
 
-    for g in range(2):
+    for g, (start, size) in enumerate(GROUPS):
         for step in (1, 7, 2, 6, 3, 5, 4):
             copy3(step, g).wait_recv()
-    total = []
-    for half in range(2):
-        value = cell(half, 0, 0, PACKED)
-        for step in range(1, NZ):
-            value = value + r3[step, half, 0:PACKED].astype(F32)
-        total.append(value)
-    roots, projection = inverse_roots(*total)
+        for half in range(2):
+            value = cell(half, 0, start, size)
+            for step in range(1, NZ):
+                value = value + r3[step, g, half, 0:size].astype(F32)
+            total[half, start : start + size] = value
+    roots, projection = inverse_roots(total[0, 0:PACKED], total[1, 0:PACKED])
 
     spread = (jnp.sqrt(F32(MEMBERS - 1.0)) * roots).astype(BF16)
     result = jnp.dot(stacked(spread), pert_s[...], preferred_element_type=F32)
@@ -374,12 +373,26 @@
     rows_copy.wait_send()
     for i in range(CHUNKS):
         flat_copy(i).wait_send()
-    for g in range(2):
+    for g in range(len(GROUPS)):
         for q in order:
             copy1(q, g).wait_send()
             copy2(q, g).wait_send()
         for step in range(1, NZ):
             copy3(step, g).wait_send()
+
+
+def results(arrived_ref, mean_ref, out_hbm, mean_hbm, wide, turned, sem):
+    copies = [pltpu.make_async_copy(mean_ref, mean_hbm, sem.at[8])]
+    copies[0].start()
+    for j in range(8):
+        lanes = pl.ds(j * 128, 128)
+        for g in range(16):
+            wide[j, pl.ds(g, 8, stride=16), :] = arrived_ref[g, :, lanes].astype(F32)
+        turned[:, :, lanes] = wide[j].reshape(8, 16, 128).astype(BF16)
+        copies.append(pltpu.make_async_copy(turned.at[:, :, lanes], out_hbm.at[:, :, lanes], sem.at[j]))
+        copies[-1].start()
+    for copy in copies:
+        copy.wait()
 
 
 def body(ensemble, obs_members, obs_values, obs_weight, obs_count, obs_tile, obs_block, obs_turn):
@@ -393,7 +406,7 @@
             jax.ShapeDtypeStruct((8, 2, 8, 1024), BF16),
             jax.ShapeDtypeStruct((2, 1024), BF16),
         ),
-        in_specs=[whole] * 8,
+        in_specs=[pl.BlockSpec(memory_space=pltpu.HBM)] * 8,
         out_specs=(whole, whole),
         scratch_shapes=[
             vmem((8, 16, 1024), BF16),
@@ -422,33 +435,49 @@
             vmem((8, PACKED, 8, 128), BF16),
             vmem((8, PACKED, 8, 128), BF16),
             vmem((2 * PACKED, 8, 128), F32),
-            vmem((NZ, 2, 24, 128), BF16),
-            vmem((NZ, 2, 24, 128), BF16),
+            vmem((NZ, len(GROUPS), 2, 8, 128), BF16),
+            vmem((NZ, len(GROUPS), 2, 8, 128), BF16),
+            vmem((2, 24, 128), F32),
             vmem((8, 2, 8, 1024), BF16),
             dma((CHUNKS,)), dma((7,)),
             dma((8,)), dma((8,)),
             dma((CHUNKS + 1,)), dma((CHUNKS + 1,)),
-            dma((16,)), dma((16,)),
-            dma((16,)), dma((16,)),
-            dma((16,)), dma((16,)),
+            dma((8 * len(GROUPS),)), dma((8 * len(GROUPS),)),
+            dma((8 * len(GROUPS),)), dma((8 * len(GROUPS),)),
+            dma((8 * len(GROUPS),)), dma((8 * len(GROUPS),)),
             dma((8,)), dma((8,)),
             dma((2,)),
         ],
         compiler_params=pltpu.CompilerParams(
-            collective_id=0, has_side_effects=True, vmem_limit_bytes=67043328
+            collective_id=0, has_side_effects=True, vmem_limit_bytes=48 << 20
         ),
     )(
-        ensemble,
-        obs_members,
-        obs_values,
-        obs_weight,
-        obs_count.reshape(1, OBD),
-        obs_tile.reshape(1, OBD),
-        obs_block.reshape(1, OBD),
-        obs_turn.reshape(1, OBD),
+        *(
+            pltpu.with_memory_space_constraint(v, pltpu.HBM)
+            for v in (
+                ensemble,
+                obs_members,
+                obs_values,
+                obs_weight,
+                obs_count.reshape(1, OBD),
+                obs_tile.reshape(1, OBD),
+                obs_block.reshape(1, OBD),
+                obs_turn.reshape(1, OBD),
+            )
+        )
     )
-    analysis = jnp.transpose(arrived.reshape(16, 8, 1024), (1, 0, 2))
-    return analysis, mean
+    return pl.pallas_call(
+        results,
+        name="results",
+        out_shape=(
+            jax.ShapeDtypeStruct((8, 16, 1024), BF16),
+            jax.ShapeDtypeStruct((2, 1024), BF16),
+        ),
+        in_specs=[pl.BlockSpec(memory_space=pltpu.VMEM)] * 2,
+        out_specs=(whole, whole),
+        scratch_shapes=[vmem((8, 128, 128), F32), vmem((8, 16, 1024), BF16), dma((9,))],
+        compiler_params=pltpu.CompilerParams(vmem_limit_bytes=16 << 20),
+    )(arrived.reshape(16, 8, 1024), mean)
 
 
 def solution(mesh):

time: 44.7 us -> 41.5 us (0.928)
  local copies, waits for them, and re-layouts: 3.08 us -> 0 us
    reshape x1 -> x0, local copies, waits for them, and re-layouts: 1.8 us -> none  [body(): analysis = jnp.transpose(arrived.reshape(16, 8, 1024), (1, 0, 2))]
    unnamed x1 -> x0, local copies, waits for them, and re-layouts: 1.28 us -> none
    pallas_call x1, Pallas kernels: 40.8 us -> 39.8 us  [body(): pl.pallas_call(kernel, name='letkf', out_shape=(jax.ShapeDtypeStruct((8,...]
    pallas_call x0 -> x1, Pallas kernels: none -> 0.92 us  [body(): pl.pallas_call(results, name='results', out_shape=(jax.ShapeDtypeStruct((...]
where the time goes in v3:
time: 41.5 us; the launch traced here: 41.4 us
  Pallas kernels  40.7 us (98%)
  between operations  0.64 us (2%)
    pallas_call x1, Pallas kernels, body(): pl.pallas_call(kernel, name='letkf', out_shape=(jax.ShapeDtypeStruct((8,...  39.8 us
    pallas_call x1, Pallas kernels, body(): pl.pallas_call(results, name='results', out_shape=(jax.ShapeDtypeStruct((...  0.92 us

profile of v3, /device:TPU:1, one launch (start us, length us, event | category | flops | bytes accessed | tf_op | source)
XLA Modules:
  0.0 41.4 jit_solution(6301017025829160549)
XLA Ops:
  0.6 39.8 %letkf.1 = (bf16[8,2,8,1024]{3,2,1,0:T(8,128)(2,1)S(1)}, bf16[2,1024]{1,0:T(2,128)(2,1)S(1)}) custom-call(bf16[8,16,1024]{2,1,0:T(8,128)(2,1)} %ens_hbm.1, bf16[128,64,128]{2,1,0:T(8,128)(2,1)} %members_hbm.1, f32[128,128]{1,0:T(8,128)} %values_hbm.1, f32[128,128]{1,0:T(8,128)} %weight_hbm.1, s32[1,128]{1,0:T(1,128)} %bitcast.6, s32[1,128]{1,0:T(1,128)} %bitcast.7, ...), custom_call_target="tpu_custom_call" | custom-call | tf_op jit(solution)/shard_map/letkf/pallas_call | solution.py:402
  40.4 0.9 %results.1 = (bf16[8,16,1024]{2,1,0:T(8,128)(2,1)}, bf16[2,1024]{1,0:T(2,128)(2,1)}) custom-call(bf16[16,8,1024]{2,1,0:T(8,128)(2,1)S(1)} %bitcast.5, bf16[2,1024]{1,0:T(2,128)(2,1)S(1)} %get-tuple-element.5.mean_ref), custom_call_target="tpu_custom_call" | custom-call | tf_op jit(solution)/shard_map/results/pallas_call | solution.py:469

commit v4 on v3

--- a/solution.py
+++ b/solution.py
@@ -16,6 +16,7 @@
 PACKED = 17
 F32, BF16 = jnp.float32, jnp.bfloat16
 CHUNKS = 8
+UNITS = (15, 9, 10, 11, 12, 0, 1, 6, 13, 5, 8, 7, 14, 4, 3, 2)
 GROUPS = ((0, 6), (6, 6), (12, 5))
 EARLY = 5
 
@@ -37,8 +38,11 @@
     half = new_col & 1
     dz = ((tile // 4) + NZ - z) & 7
     dx = ((tile & 3) + NX - x) & 3
-    inner = jnp.where(half == 0, dy * 32 + dx * 8, dx * 32 + dy * 8) + dz
-    return dc * 256 + half * 128 + inner
+    place = dy * NX + dx
+    unit = jnp.zeros_like(place)
+    for k, value in enumerate(UNITS):
+        unit = unit + jnp.where(place == k, value, 0)
+    return dc * 256 + unit * 16 + half * 8 + dz
 
 
 def beside(left, right):
@@ -114,32 +118,9 @@
     out_hbm, mean_hbm,
     ens_ref, values_ref, weight_ref, count_ref, tile_ref, block_ref, turn_ref, mean_ref,
     obs, ens_f, ens_s, ens_r, means, pert_s, root_s, flat_f, flat_s, flat_r, rows_s, rows_r,
-    s1, r1, acc1, s2, r2, acc2, s3, r3, total, ana,
+    s1, r1, far1, near1, acc1, s2, r2, acc2, s3, r3, total, ana,
     load_sem, small_sem, ens_ss, ens_rs, flat_ss, flat_rs, ss1, rs1, ss2, rs2, ss3, rs3, out_ss, out_rs, own_sem,
 ):
-    t, m = lax.axis_index("tile"), lax.axis_index("mem")
-    z, x, y, c = t // 4, t % 4, m // 2, m % 2
-
-    def at_mem(step):
-        return (t, lax.rem(m + step, 8))
-
-    def at_core():
-        return (t, y * 2 + 1 - c)
-
-    def at_y(step):
-        return (t, lax.rem(y + step, NY) * 2 + c)
-
-    def at_x(step):
-        return (z * 4 + lax.rem(x + step, NX), m)
-
-    def at_z(step):
-        return (lax.rem(z + step, NZ) * 4 + x, m)
-
-    def remote(src, dst, send_sem, recv_sem, device):
-        return pltpu.make_async_remote_copy(
-            src_ref=src, dst_ref=dst, send_sem=send_sem, recv_sem=recv_sem, device_id=device, device_id_type=MESH
-        )
-
     per = OBD // CHUNKS
 
     def load(i):
@@ -167,6 +148,29 @@
     for copy in small[3:]:
         copy.start()
 
+    t, m = lax.axis_index("tile"), lax.axis_index("mem")
+    z, x, y, c = lax.div(t, 4), lax.rem(t, 4), lax.div(m, 2), lax.rem(m, 2)
+
+    def at_mem(step):
+        return (t, lax.rem(m + step, 8))
+
+    def at_core():
+        return (t, y * 2 + 1 - c)
+
+    def at_y(step):
+        return (t, lax.rem(y + step, NY) * 2 + c)
+
+    def at_x(step):
+        return (z * 4 + lax.rem(x + step, NX), m)
+
+    def at_z(step):
+        return (lax.rem(z + step, NZ) * 4 + x, m)
+
+    def remote(src, dst, send_sem, recv_sem, device):
+        return pltpu.make_async_remote_copy(
+            src_ref=src, dst_ref=dst, send_sem=send_sem, recv_sem=recv_sem, device_id=device, device_id_type=MESH
+        )
+
     barrier = pltpu.get_barrier_semaphore()
     partners = [at_mem(s) for s in range(1, 8)] + [at_x(s) for s in range(1, NX)] + [at_z(s) for s in range(1, NZ)]
     for device in partners:
@@ -220,15 +224,16 @@
 
     lax.fori_loop(0, EARLY, plain, 0)
 
-    for copy in small[3:]:
+    for copy in small[3:6]:
         copy.wait()
     rows = cell_rows(tile_ref[...], block_ref[...], turn_ref[...], z, x, y, c).astype(F32)
     rows_s[...] = jnp.broadcast_to(rows - 256.0, (8, OBD))
+
+    small[6].wait()
     for j in range(8):
         for k in range(8):
             ens_f[j, pl.ds(k, 16, stride=8), :] = ens_ref[k, :, j * 128 : j * 128 + 128].astype(F32)
         ens_s[:, :, :, j * 128 : j * 128 + 128] = ens_f[j].reshape(8, 2, 8, 128).astype(BF16)
-
     pl.semaphore_wait(barrier, len(partners))
     rows_copy = remote(rows_s, rows_r, flat_ss.at[CHUNKS], flat_rs.at[CHUNKS], at_core())
     rows_copy.start()
@@ -250,12 +255,12 @@
     )
 
     def keep(r, sums):
-        for q in range(8):
-            part = sums[q * 32 : q * 32 + 32]
-            if q % 4:
-                s1[q, r] = part.astype(BF16)
-            else:
-                acc1[q // 4, r] = part
+        for q in range(4):
+            s1[q, r] = sums[q * 32 : q * 32 + 32].astype(BF16)
+        far1[0, r] = sums[128:136].astype(BF16)
+        far1[1, r] = sums[136:144].astype(BF16)
+        for k in range(7):
+            acc1[k, r] = sums[144 + k * 16 : 160 + k * 16]
 
     def both_cores(r):
         return jnp.concatenate([flat_s[:, r].reshape(OBD, 128), flat_r[:, r].reshape(OBD, 128)], axis=0)
@@ -269,21 +274,21 @@
 
     def copy1(q, g):
         span = pl.ds(*GROUPS[g])
-        at, step = q * len(GROUPS) + g, q % 4
-        device = at_x(step) if q >= 4 else at_y(step)
-        return remote(s1.at[q, span], r1.at[q, span], ss1.at[at], rs1.at[at], device)
+        at = q * len(GROUPS) + g
+        device = (at_y(1), at_y(3), at_x(1), at_x(3), at_y(2), at_x(2))[q]
+        source, target = (s1.at[q, span], r1.at[q, span]) if q < 4 else (far1.at[q - 4, span], near1.at[q - 4, span])
+        return remote(source, target, ss1.at[at], rs1.at[at], device)
 
     def copy2(q, g):
         span = pl.ds(*GROUPS[g])
-        at, step = q * len(GROUPS) + g, q % 4
-        device = at_y(step) if q >= 4 else at_x(step)
-        return remote(s2.at[q, span], r2.at[q, span], ss2.at[at], rs2.at[at], device)
+        at = q * len(GROUPS) + g
+        return remote(s2.at[q, span], r2.at[q, span], ss2.at[at], rs2.at[at], at_x(q + 1) if q < 3 else at_y(q - 2))
 
     def copy3(step, g):
         at = step * len(GROUPS) + g
         return remote(s3.at[step, g], r3.at[step, g], ss3.at[at], rs3.at[at], at_z(step))
 
-    order = (2, 6, 1, 5, 3, 7)
+    order = (4, 5, 0, 1, 2, 3)
     for g, (start, size) in enumerate(GROUPS):
         lax.fori_loop(start // 2, (start + size) // 2, pair, 0)
         if size % 2:
@@ -293,17 +298,25 @@
 
     for g, (start, size) in enumerate(GROUPS):
         span = pl.ds(start, size)
-        for half in range(2):
-            for step in (1, 3, 2):
-                copy1(half * 4 + step, g).wait_recv()
-            acc = acc1[half, span]
-            for step in range(1, 4):
-                acc = acc + r1[half * 4 + step, span].astype(F32)
-            acc2[pl.ds(half * PACKED + start, size)] = acc[:, 0:8]
-            for step in (2, 1, 3):
-                q = half * 4 + step
-                s2[q, span] = acc[:, step * 8 : step * 8 + 8].astype(BF16)
-                copy2(q, g).start()
+        for q in range(4):
+            copy1(q, g).wait_recv()
+
+        def come(q, unit, span=span):
+            return r1[q, span, unit * 16 : unit * 16 + 16].astype(F32)
+
+        for q, source, unit in ((0, 0, 0), (2, 1, 0), (3, 3, 0), (5, 2, 0)):
+            s2[q, span] = (acc1[q, span] + come(source, unit)).astype(BF16)
+            copy2(q, g).start()
+        for q in (4, 5):
+            copy1(q, g).wait_recv()
+        for axis, (q, one, two) in enumerate(((1, 0, 1), (4, 2, 3))):
+            value = acc1[q, span] + come(one, 1) + come(two, 1)
+            far = near1[axis, span].astype(F32)
+            parts = [value[:, 0:8], value[:, 8:16]]
+            parts[axis] = parts[axis] + far
+            s2[q, span, 0:8] = parts[0].astype(BF16)
+            s2[q, span, 8:16] = parts[1].astype(BF16)
+            copy2(q, g).start()
 
     wide = acc2.reshape(2 * PACKED * 8, 128)
 
@@ -311,14 +324,12 @@
         return wide[pl.ds((half * PACKED + start) * 8 + step, size, stride=8), :]
 
     for g, (start, size) in enumerate(GROUPS):
+        value = acc1[6, pl.ds(start, size)]
+        for q in (0, 2, 3, 5, 1, 4):
+            copy2(q, g).wait_recv()
+            value = value + r2[q, pl.ds(start, size)].astype(F32)
         for half in range(2):
-            for step in (1, 3, 2):
-                copy2(half * 4 + step, g).wait_recv()
-            span = pl.ds(half * PACKED + start, size)
-            acc = acc2[span]
-            for step in range(1, 4):
-                acc = acc + r2[half * 4 + step, pl.ds(start, size)].astype(F32)
-            acc2[span] = acc
+            acc2[pl.ds(half * PACKED + start, size)] = value[:, half * 8 : half * 8 + 8]
         for step in (4, 3, 5, 2, 6, 1, 7):
             for half in range(2):
                 s3[step, g, half, 0:size] = cell(half, step, start, size).astype(BF16)
@@ -364,10 +375,6 @@
     mean_copy = pltpu.make_async_copy(mean_ref, mean_hbm, own_sem.at[1])
     mean_copy.start()
 
-    for copy in out_copies:
-        copy.wait()
-    mine.wait()
-    mean_copy.wait()
     for copy in ens_copies:
         copy.wait_send()
     rows_copy.wait_send()
@@ -379,6 +386,10 @@
             copy2(q, g).wait_send()
         for step in range(1, NZ):
             copy3(step, g).wait_send()
+    for copy in out_copies:
+        copy.wait()
+    mine.wait()
+    mean_copy.wait()
 
 
 def results(arrived_ref, mean_ref, out_hbm, mean_hbm, wide, turned, sem):
@@ -429,11 +440,13 @@
             vmem((CHUNKS, PACKED, per, 128), BF16),
             vmem((8, OBD), F32),
             vmem((8, OBD), F32),
-            vmem((8, PACKED, 32, 128), BF16),
-            vmem((8, PACKED, 32, 128), BF16),
-            vmem((2, PACKED, 32, 128), F32),
-            vmem((8, PACKED, 8, 128), BF16),
-            vmem((8, PACKED, 8, 128), BF16),
+            vmem((4, PACKED, 32, 128), BF16),
+            vmem((4, PACKED, 32, 128), BF16),
+            vmem((2, PACKED, 8, 128), BF16),
+            vmem((2, PACKED, 8, 128), BF16),
+            vmem((7, PACKED, 16, 128), F32),
+            vmem((6, PACKED, 16, 128), BF16),
+            vmem((6, PACKED, 16, 128), BF16),
             vmem((2 * PACKED, 8, 128), F32),
             vmem((NZ, len(GROUPS), 2, 8, 128), BF16),
             vmem((NZ, len(GROUPS), 2, 8, 128), BF16),

time: 41.5 us -> 39.3 us (0.947)
  Pallas kernels: 40.7 us -> 38.6 us
    pallas_call x1, Pallas kernels: 39.8 us -> 37.7 us  [body(): pl.pallas_call(kernel, name='letkf', out_shape=(jax.ShapeDtypeStruct((8,...]
where the time goes in v4:
time: 39.3 us; the launch traced here: 39.2 us
  Pallas kernels  38.6 us (98%)
  between operations  0.64 us (2%)
    pallas_call x1, Pallas kernels, body(): pl.pallas_call(kernel, name='letkf', out_shape=(jax.ShapeDtypeStruct((8,...  37.7 us
    pallas_call x1, Pallas kernels, body(): pl.pallas_call(results, name='results', out_shape=(jax.ShapeDtypeStruct((...  0.92 us

profile of v4, /device:TPU:1, one launch (start us, length us, event | category | flops | bytes accessed | tf_op | source)
XLA Modules:
  0.0 39.2 jit_solution(17388704461329494888)
XLA Ops:
  0.6 37.7 %letkf.1 = (bf16[8,2,8,1024]{3,2,1,0:T(8,128)(2,1)S(1)}, bf16[2,1024]{1,0:T(2,128)(2,1)S(1)}) custom-call(bf16[8,16,1024]{2,1,0:T(8,128)(2,1)} %ens_hbm.1, bf16[128,64,128]{2,1,0:T(8,128)(2,1)} %members_hbm.1, f32[128,128]{1,0:T(8,128)} %values_hbm.1, f32[128,128]{1,0:T(8,128)} %weight_hbm.1, s32[1,128]{1,0:T(1,128)} %bitcast.6, s32[1,128]{1,0:T(1,128)} %bitcast.7, ...), custom_call_target="tpu_custom_call" | custom-call | tf_op jit(solution)/shard_map/letkf/pallas_call | solution.py:413
  38.3 0.9 %results.1 = (bf16[8,16,1024]{2,1,0:T(8,128)(2,1)}, bf16[2,1024]{1,0:T(2,128)(2,1)}) custom-call(bf16[16,8,1024]{2,1,0:T(8,128)(2,1)S(1)} %bitcast.5, bf16[2,1024]{1,0:T(2,128)(2,1)S(1)} %get-tuple-element.5.mean_ref), custom_call_target="tpu_custom_call" | custom-call | tf_op jit(solution)/shard_map/results/pallas_call | solution.py:482

commit v5 on v4

--- a/solution.py
+++ b/solution.py
@@ -17,7 +17,7 @@
 F32, BF16 = jnp.float32, jnp.bfloat16
 CHUNKS = 8
 UNITS = (15, 9, 10, 11, 12, 0, 1, 6, 13, 5, 8, 7, 14, 4, 3, 2)
-GROUPS = ((0, 6), (6, 6), (12, 5))
+GROUPS = ((0, 4), (4, 6), (10, 7))
 EARLY = 5
 
 
@@ -298,13 +298,11 @@
 
     for g, (start, size) in enumerate(GROUPS):
         span = pl.ds(start, size)
-        for q in range(4):
-            copy1(q, g).wait_recv()
-
         def come(q, unit, span=span):
             return r1[q, span, unit * 16 : unit * 16 + 16].astype(F32)
 
-        for q, source, unit in ((0, 0, 0), (2, 1, 0), (3, 3, 0), (5, 2, 0)):
+        for q, source, unit in ((0, 0, 0), (3, 3, 0), (2, 1, 0), (5, 2, 0)):
+            copy1(source, g).wait_recv()
             s2[q, span] = (acc1[q, span] + come(source, unit)).astype(BF16)
             copy2(q, g).start()
         for q in (4, 5):

time: 39.3 us -> 39.2 us (level)
  no operation moved by 1% of the time
where the time goes in v5:
time: 39.2 us; the launch traced here: 39.1 us
  Pallas kernels  38.5 us (98%)
  between operations  0.64 us (2%)
    pallas_call x1, Pallas kernels, body(): pl.pallas_call(kernel, name='letkf', out_shape=(jax.ShapeDtypeStruct((8,...  37.6 us
    pallas_call x1, Pallas kernels, body(): pl.pallas_call(results, name='results', out_shape=(jax.ShapeDtypeStruct((...  0.92 us

profile of v5, /device:TPU:1, one launch (start us, length us, event | category | flops | bytes accessed | tf_op | source)
XLA Modules:
  0.0 39.1 jit_solution(16871508177253266797)
XLA Ops:
  0.6 37.6 %letkf.1 = (bf16[8,2,8,1024]{3,2,1,0:T(8,128)(2,1)S(1)}, bf16[2,1024]{1,0:T(2,128)(2,1)S(1)}) custom-call(bf16[8,16,1024]{2,1,0:T(8,128)(2,1)} %ens_hbm.1, bf16[128,64,128]{2,1,0:T(8,128)(2,1)} %members_hbm.1, f32[128,128]{1,0:T(8,128)} %values_hbm.1, f32[128,128]{1,0:T(8,128)} %weight_hbm.1, s32[1,128]{1,0:T(1,128)} %bitcast.6, s32[1,128]{1,0:T(1,128)} %bitcast.7, ...), custom_call_target="tpu_custom_call" | custom-call | tf_op jit(solution)/shard_map/letkf/pallas_call | solution.py:411
  38.2 0.9 %results.1 = (bf16[8,16,1024]{2,1,0:T(8,128)(2,1)}, bf16[2,1024]{1,0:T(2,128)(2,1)}) custom-call(bf16[16,8,1024]{2,1,0:T(8,128)(2,1)S(1)} %bitcast.5, bf16[2,1024]{1,0:T(2,128)(2,1)S(1)} %get-tuple-element.5.mean_ref), custom_call_target="tpu_custom_call" | custom-call | tf_op jit(solution)/shard_map/results/pallas_call | solution.py:480
